TPU v7x, 32 devices: a whole 2x2x4 slice. The times are simulated.
32 devices in a mesh: dp: 4 (over y, x), tile: 8 (over z, core).
Axes of the slice: x: 2, y: 2, z: 4, core: 2. Of those that a mesh axis runs over, the one named last changes fastest.
Arguments:
- features: bfloat16 [4, 8, 512, 1280], P('dp', 'tile'), may hold values from -6 to 6
- visible: int32 [4, 8, 512], P('dp', 'tile'), may hold values from 0 to 1, as said below
- positions: int32 [4, 8, 512], P('dp', 'tile'), may hold values from 0 to 511, each once within a row
- cotangent: bfloat16 [4, 8, 512, 512], P('dp', 'tile'), may hold values from -6 to 6
- mlp_gain: float32 [1280], replicated, may hold values from 0.1 to 1.9
- mlp_bias: float32 [1280], replicated, may hold values from -3 to 3
- fc1_weight: bfloat16 [1280, 2560], replicated, may hold values from -0.15625 to 0.15625
- fc1_bias: float32 [2560], replicated, may hold values from -3 to 3
- fc2_weight: bfloat16 [2560, 1280], replicated, may hold values from -0.125 to 0.125
- fc2_bias: float32 [1280], replicated, may hold values from -3 to 3
- encoder_gain: float32 [1280], replicated, may hold values from 0.1 to 1.9
- encoder_bias: float32 [1280], replicated, may hold values from -3 to 3
- embed_weight: bfloat16 [1280, 512], replicated, may hold values from -0.15625 to 0.15625
- embed_bias: float32 [512], replicated, may hold values from -3 to 3
- mask_token: float32 [512], replicated, may hold values from -4 to 4
- position_table: bfloat16 [512, 512], replicated, may hold values from -4 to 4
- decoder_gain: float32 [512], replicated, may hold values from 0.1 to 1.9
- decoder_bias: float32 [512], replicated, may hold values from -3 to 3
Outputs:
- feature_grad: bfloat16 [4, 8, 512, 1280], P('dp', 'tile')
- decoded: bfloat16 [4, 8, 512, 512], P('dp', 'tile')
- fc1_grad: float32 [1280, 2560], P('tile')
- fc2_grad: float32 [2560, 1280], P('tile')
Inputs may be any that keep to these rules, and one draw needn't show every extreme that they name: In each scene (all 8 chips of one index of the first dimension) exactly 1024 patches are visible; each chip has at most 256 visible patches, and in every scene one chip has exactly 256. Each chip's position ids are a permutation of its 512 positions.
All inputs are finite; a program needn't handle non-finite values.
Results may differ from a plain program's by a relative error of at most 0.007.
Values may be sent and summed in bfloat16 or wider, within the bound.
A program may use at most 128 MiB of HBM per device.

v0:
```python
import jax
import jax.numpy as jnp
from jax import lax
from jax.sharding import PartitionSpec as P

epsilon = 1e-06


def layer_norm(values, norm_gain, norm_bias):
    row_mean = jnp.mean(values, axis=-1, keepdims=True)
    centred = values - row_mean
    variance = jnp.mean(centred * centred, axis=-1, keepdims=True)
    inv_std = lax.rsqrt(variance + epsilon)
    scaled = centred * inv_std
    return (scaled * norm_gain + norm_bias, scaled, inv_std)


def norm_back(upstream, scaled, inv_std):
    mean_up = jnp.mean(upstream, axis=-1, keepdims=True)
    mean_cross = jnp.mean(upstream * scaled, axis=-1, keepdims=True)
    return inv_std * (upstream - mean_up - scaled * mean_cross)


def gelu_parts(pre_act):
    normal_cdf = 0.5 * (1.0 + lax.erf(pre_act * 0.7071067811865476))
    density = jnp.exp(-0.5 * pre_act * pre_act) * 0.3989422804014327
    return (pre_act * normal_cdf, normal_cdf + pre_act * density)


def encode(enc_input, enc_params):
    (
        mlp_gain,
        mlp_bias,
        fc1_weight,
        fc1_bias,
        fc2_weight,
        fc2_bias,
        encoder_gain,
        encoder_bias,
        embed_weight,
        embed_bias,
    ) = enc_params
    rows_in = enc_input.astype(jnp.float32)
    mlp_in, mlp_scaled, mlp_inv = layer_norm(rows_in, mlp_gain, mlp_bias)
    mlp_in = mlp_in.astype(jnp.bfloat16)
    pre_act = jnp.dot(mlp_in, fc1_weight, preferred_element_type=jnp.float32) + fc1_bias
    activation, slope = gelu_parts(pre_act)
    hidden = activation.astype(jnp.bfloat16)
    encoded = rows_in + jnp.dot(hidden, fc2_weight, preferred_element_type=jnp.float32) + fc2_bias
    normed, enc_scaled, enc_inv = layer_norm(encoded, encoder_gain, encoder_bias)
    normed = normed.astype(jnp.bfloat16)
    projected = (
        jnp.dot(normed, embed_weight, preferred_element_type=jnp.float32) + embed_bias
    ).astype(jnp.bfloat16)
    saved = (mlp_in, mlp_scaled, mlp_inv, slope, hidden, enc_scaled, enc_inv)
    return (saved, projected)


def encode_back(saved, grad_compact, enc_params):
    (
        mlp_gain,
        mlp_bias,
        fc1_weight,
        fc1_bias,
        fc2_weight,
        fc2_bias,
        encoder_gain,
        encoder_bias,
        embed_weight,
        embed_bias,
    ) = enc_params
    mlp_in, mlp_scaled, mlp_inv, slope, hidden, enc_scaled, enc_inv = saved
    grad_normed = jnp.dot(grad_compact, embed_weight.T, preferred_element_type=jnp.float32)
    grad_encoded = norm_back(grad_normed * encoder_gain, enc_scaled, enc_inv).astype(jnp.bfloat16)
    grad_hidden = jnp.dot(grad_encoded, fc2_weight.T, preferred_element_type=jnp.float32)
    grad_pre = (grad_hidden * slope).astype(jnp.bfloat16)
    grad_mlp_in = jnp.dot(grad_pre, fc1_weight.T, preferred_element_type=jnp.float32)
    grad_feats = (
        grad_encoded.astype(jnp.float32) + norm_back(grad_mlp_in * mlp_gain, mlp_scaled, mlp_inv)
    ).astype(jnp.bfloat16)
    fc1_term = jnp.dot(mlp_in.T, grad_pre, preferred_element_type=jnp.float32)
    fc2_term = jnp.dot(hidden.T, grad_encoded, preferred_element_type=jnp.float32)
    return (fc1_term, fc2_term, grad_feats)


def decoder_pass(
    projected_rows,
    keep_rows,
    position_ids,
    upstream,
    position_table,
    mask_token,
    decoder_gain,
    decoder_bias,
):
    placed = jnp.take(position_table, position_ids, axis=0).astype(jnp.float32)
    dec_input = jnp.where(keep_rows, projected_rows.astype(jnp.float32), mask_token) + placed
    decoded, dec_scaled, dec_inv = layer_norm(dec_input, decoder_gain, decoder_bias)
    grad_input = norm_back(upstream.astype(jnp.float32) * decoder_gain, dec_scaled, dec_inv)
    grad_projected = jnp.where(keep_rows, grad_input, 0.0).astype(jnp.bfloat16)
    return (decoded.astype(jnp.bfloat16), grad_projected)


def spread(source_rows, indices, valid, lead_shape):
    picked = jnp.take(source_rows, indices, axis=0).reshape(lead_shape + (source_rows.shape[1],))
    return jnp.where(valid, picked, jnp.zeros((), source_rows.dtype))


def shards(
    features,
    visible,
    positions,
    cotangent,
    mlp_gain,
    mlp_bias,
    fc1_weight,
    fc1_bias,
    fc2_weight,
    fc2_bias,
    encoder_gain,
    encoder_bias,
    embed_weight,
    embed_bias,
    mask_token,
    position_table,
    decoder_gain,
    decoder_bias,
):
    scene_count = features.shape[0]
    patch_count = features.shape[2]
    model_width = features.shape[3]
    dec_width = embed_weight.shape[1]
    total_rows = scene_count * patch_count
    vis_flags = visible.reshape(scene_count, patch_count)
    row_data = features.reshape(total_rows, model_width)
    keep_rows = (vis_flags.reshape(-1) > 0)[:, None]
    position_ids = positions.reshape(-1)
    upstream = cotangent.reshape(total_rows, dec_width)
    counts = jnp.sum(vis_flags, axis=1)
    row_rank = jnp.cumsum(vis_flags, axis=1) - vis_flags
    scene_col = jnp.arange(scene_count, dtype=jnp.int32)[:, None]
    target = jnp.where(vis_flags > 0, scene_col * patch_count + row_rank, total_rows)
    row_order = (
        jnp.zeros((total_rows,), jnp.int32)
        .at[target.reshape(-1)]
        .set(jnp.arange(total_rows, dtype=jnp.int32), mode="drop")
    )
    most_rows = patch_count // 2
    enc_params = (
        mlp_gain,
        mlp_bias,
        fc1_weight,
        fc1_bias,
        fc2_weight,
        fc2_bias,
        encoder_gain,
        encoder_bias,
        embed_weight,
        embed_bias,
    )
    decoder_args = (position_table, mask_token, decoder_gain, decoder_bias)
    tile_count = lax.axis_size("tile")
    capacity = most_rows // tile_count
    share_rows = patch_count // 4
    lead_shape = (tile_count, scene_count, capacity)
    all_counts = lax.all_gather(counts[None, :], "tile", axis=0, tiled=True)
    run_ends = jnp.cumsum(all_counts, axis=0)
    starts = run_ends - all_counts
    my_tile = lax.axis_index("tile")
    own_start = lax.dynamic_index_in_dim(starts, my_tile, 0, keepdims=False)
    peer_ids = jnp.arange(tile_count, dtype=jnp.int32)[:, None, None]
    scene_ids = jnp.arange(scene_count, dtype=jnp.int32)[None, :, None]
    column_ids = jnp.arange(capacity, dtype=jnp.int32)[None, None, :]
    send_rank = column_ids * tile_count + jnp.mod(peer_ids - own_start[None, :, None], tile_count)
    send_valid = (send_rank < counts[None, :, None])[..., None]
    send_rows = row_order[
        (scene_ids * patch_count + jnp.minimum(send_rank, patch_count - 1)).reshape(-1)
    ]
    home_peer = jnp.mod(own_start[:, None] + row_rank, tile_count)
    home_index = (
        (home_peer * scene_count + scene_col) * capacity
        + jnp.minimum(row_rank // tile_count, capacity - 1)
    ).reshape(-1)
    slot_ids = jnp.arange(share_rows, dtype=jnp.int32)[None, :]
    global_pos = my_tile + tile_count * slot_ids
    source = jnp.sum((run_ends[:, :, None] <= global_pos[None]).astype(jnp.int32), axis=0)
    source = jnp.minimum(source, tile_count - 1)
    source_start = jnp.sum(jnp.where(peer_ids == source[None], starts[:, :, None], 0), axis=0)
    enc_rows = (
        (source * scene_count + scene_col) * capacity
        + jnp.minimum((global_pos - source_start) // tile_count, capacity - 1)
    ).reshape(-1)
    peer_start = starts[:, :, None]
    back_rank = column_ids * tile_count + jnp.mod(my_tile - peer_start, tile_count)
    back_valid = (back_rank < all_counts[:, :, None])[..., None]
    back_slot = jnp.minimum((peer_start + back_rank) // tile_count, share_rows - 1)
    back_rows = (scene_ids * share_rows + back_slot).reshape(-1)
    incoming = lax.all_to_all(
        spread(row_data, send_rows, send_valid, lead_shape),
        "tile",
        split_axis=0,
        concat_axis=0,
        tiled=True,
    )
    enc_input = jnp.take(incoming.reshape(-1, model_width), enc_rows, axis=0)
    saved, projected = encode(enc_input, enc_params)
    returned = lax.all_to_all(
        spread(projected, back_rows, back_valid, lead_shape),
        "tile",
        split_axis=0,
        concat_axis=0,
        tiled=True,
    )
    projected_rows = jnp.where(
        keep_rows, jnp.take(returned.reshape(-1, dec_width), home_index, axis=0), 0
    )
    decoded, grad_projected = decoder_pass(
        projected_rows, keep_rows, position_ids, upstream, *decoder_args
    )
    grad_arrived = lax.all_to_all(
        spread(grad_projected, send_rows, send_valid, lead_shape),
        "tile",
        split_axis=0,
        concat_axis=0,
        tiled=True,
    )
    grad_compact = jnp.take(grad_arrived.reshape(-1, dec_width), enc_rows, axis=0)
    fc1_term, fc2_term, grad_feats = encode_back(saved, grad_compact, enc_params)
    feats_back = lax.all_to_all(
        spread(grad_feats, back_rows, back_valid, lead_shape),
        "tile",
        split_axis=0,
        concat_axis=0,
        tiled=True,
    )
    grad_rows = jnp.where(
        keep_rows, jnp.take(feats_back.reshape(-1, model_width), home_index, axis=0), 0
    )
    shares = (
        lax.psum_scatter(fc1_term, "tile", scatter_dimension=0, tiled=True),
        lax.psum_scatter(fc2_term, "tile", scatter_dimension=0, tiled=True),
    )
    totals = lax.psum((shares[0], shares[1]), "dp")
    device_total = lax.axis_size("dp") * lax.axis_size("tile")
    feature_grad = grad_rows.reshape(features.shape)
    decoded_out = decoded.reshape(cotangent.shape)
    return (feature_grad, decoded_out, totals[0] / device_total, totals[1] / device_total)


def solution(mesh):
    return jax.shard_map(
        shards,
        mesh=mesh,
        in_specs=(
            P("dp", "tile", None, None),
            P("dp", "tile", None),
            P("dp", "tile", None),
            P("dp", "tile", None, None),
            P(),
            P(),
            P(),
            P(),
            P(),
            P(),
            P(),
            P(),
            P(),
            P(),
            P(),
            P(),
            P(),
            P(),
        ),
        out_specs=(
            P("dp", "tile", None, None),
            P("dp", "tile", None, None),
            P("tile", None),
            P("tile", None),
        ),
        check_vma=False,
    )
```

profile of v0, /device:TPU:0, one launch (start us, length us, event | category | flops | bytes accessed | tf_op | source)
XLA Modules:
  0.0 478.5 jit_solution(15687220451564410560)
XLA Ops:
  7.2 1.4 reduce_sum.137
  9.9 1.4 dynamic-update-slice
  11.3 10.6 %all-reduce = s32[8]{0:T(128)S(1)} all-reduce(s32[8]{0:T(128)S(1)} %dynamic-update-slice), channel_id=1, replica_groups=mesh['dp'=4,'tile'=8] {'tile'}, use_global_device_ids=true, to_apply=%add | all-reduce | flops 8 | bytes 64
  25.0 1.4 compare_select_fusion.1
  26.3 2.4 scatter_custom_fusion
  28.8 1.9 gather_fusion
  31.6 1.2 gather_fusion.1
  33.8 3.5 all-to-all-start
  37.7 17.7 %all-to-all-done = bf16[8,1,32,1280]{3,2,1,0:T(8,128)(2,1)S(1)} async-done(((bf16[8,1,32,1280]{3,2,1,0:T(8,128)(2,1)}), bf16[8,1,32,1280]{3,2,1,0:T(8,128)(2,1)S(1)}, u32[]{:S(2)}, u32[]{:S(2)}) %all-to-all-start) | async-done | bytes 655392 | tf_op jit(solution)/shard_map/all_to_all | solution.py:198
  56.9 4.2 convolution_add_fusion
  61.5 1.3 fusion.69
  65.7 3.4 all-to-all-start.1
  69.2 2.0 gather_fusion.5
  72.0 6.8 %all-to-all-done.1 = bf16[8,1,32,512]{3,2,1,0:T(8,128)(2,1)S(1)} async-done(((bf16[8,1,32,512]{3,2,1,0:T(8,128)(2,1)}), bf16[8,1,32,512]{3,2,1,0:T(8,128)(2,1)S(1)}, u32[]{:S(2)}, u32[]{:S(2)}) %all-to-all-start.1) | async-done | bytes 262176 | tf_op jit(solution)/shard_map/all_to_all | solution.py:207
  78.8 2.0 gather_fusion.4
  84.9 12.3 %all_to_all.20 = bf16[8,1,32,512]{3,2,1,0:T(8,128)(2,1)S(1)} all-to-all(bf16[8,1,32,512]{3,2,1,0:T(8,128)(2,1)S(1)} %select_select_fusion.3), channel_id=1, replica_groups=mesh['dp'=4,'tile'=8] {'tile'}, dimensions={0} | all-to-all | bytes 524288 | tf_op jit(solution)/shard_map/all_to_all | solution.py:220
  98.1 2.0 fusion.68
  101.4 6.6 %fusion.66 = f32[2560,1280]{1,0:T(8,128)} fusion(bf16[128,1280]{1,0:T(8,128)(2,1)S(1)} %multiply_convert_fusion.1, f32[128,2560]{1,0:T(8,128)S(1)} %copy-done.4), kind=kOutput, calls=%fused_computation.200 | convolution fusion | flops 840499200 | bytes 14745600 | tf_op jit(solution)/shard_map/dot_general | solution.py:82
  109.3 5.1 %fusion = bf16[128,2560]{1,0:T(8,128)(2,1)S(1)} fusion(bf16[128,1280]{1,0:T(8,128)(2,1)S(1)} %multiply_convert_fusion.1, bf16[2560,1280]{1,0:T(8,128)(2,1)} %param.26, f32[128,2560]{1,0:T(8,128)S(1)} %copy-done.5), kind=kOutput, calls=%fused_computation.13 | convolution fusion | flops 842137600 | bytes 8847360 | tf_op jit(solution)/shard_map/dot_general | solution.py:75
  115.3 6.7 %fusion.63 = f32[1280,2560]{1,0:T(8,128)} fusion(bf16[128,2560]{1,0:T(8,128)(2,1)S(1)} %fusion, f32[1280]{0:T(1024)S(1)} %copy-done.12, f32[1280]{0:T(1024)S(1)} %copy-done.11, f32[128]{0:T(128)S(1)} %add_rsqrt_fusion.2, f32[128]{0:T(128)S(1)} %broadcast_multiply_fusion.10, bf16[128,1280]{1,0:T(8,128)(2,1)S(1)} %gather_fusion.2, ...), kind=kOutput, calls=%fused_computation.199 | convolution fusion | flops 840007680 | bytes 14101632 | tf_op jit(solution)/shard_map/dot_general | solution.py:81
  122.1 119.2 %reduce-scatter.5.cloned.1.call-done = f32[320,1280]{1,0:T(8,128)} async-done(((f32[2560,1280]{1,0:T(8,128)}), f32[320,1280]{1,0:T(8,128)}) %reduce-scatter.5.cloned.1.call-update) | async-done | bytes 1638416 | tf_op jit(solution)/shard_map/reduce_scatter | solution.py:241
  241.3 134.9 %reduce-scatter.3.cloned.1.call-done = f32[160,2560]{1,0:T(8,128)} async-done(((f32[1280,2560]{1,0:T(8,128)}), f32[160,2560]{1,0:T(8,128)}) %reduce-scatter.3.cloned.1.call-update) | async-done | bytes 1638416 | tf_op jit(solution)/shard_map/reduce_scatter | solution.py:240
  377.2 5.1 %fusion.67 = (f32[128]{0:T(128)S(1)}, f32[128]{0:T(128)S(1)}, f32[128,1280]{1,0:T(8,128)S(1)}) fusion(f32[128]{0:T(128)S(1)} %add_rsqrt_fusion.2, f32[128]{0:T(128)S(1)} %broadcast_multiply_fusion.10, bf16[128,1280]{1,0:T(8,128)(2,1)S(1)} %gather_fusion.2, pred[128]{0:T(512)(128)(4,1)S(1)} %compare_and_fusion.3, f32[1280]{0:T(1024)S(1)} %copy-done.11, ...), kind=kOutput, calls=%fused_computation.201 | convolution fusion | flops 840171264 | bytes 8199296 | tf_op jit(solution)/shard_map/dot_general | solution.py:77
  382.7 1.2 gather_fusion.8
  385.0 3.5 all-to-all-start.3
  388.5 1.4 add_convert_fusion
  389.9 16.7 %all-to-all-done.3 = bf16[8,1,32,1280]{3,2,1,0:T(8,128)(2,1)S(1)} async-done(((bf16[8,1,32,1280]{3,2,1,0:T(8,128)(2,1)}), bf16[8,1,32,1280]{3,2,1,0:T(8,128)(2,1)S(1)}, u32[]{:S(2)}, u32[]{:S(2)}) %all-to-all-start.3) | async-done | bytes 655392 | tf_op jit(solution)/shard_map/all_to_all | solution.py:229
  406.6 2.1 gather_fusion.9
  408.7 1.3 fusion.6
  410.0 57.2 %all-reduce.4.cloned.1.call-done = (f32[160,2560]{1,0:T(8,128)}, f32[320,1280]{1,0:T(8,128)}) async-done(((f32[160,2560]{1,0:T(8,128)}, f32[320,1280]{1,0:T(8,128)}), (f32[160,2560]{1,0:T(8,128)}, f32[320,1280]{1,0:T(8,128)})) %all-reduce.4.cloned.1.call-update) | async-done | bytes 3276816 | tf_op jit(solution)/shard_map/psum | solution.py:243
  467.3 2.8 broadcast_multiply_fusion.1
  470.1 1.3 broadcast_multiply_fusion
  (122 shorter events, 23.4 us)
Async XLA Ops:
  7.2 24.4 %copy-start = (bf16[1,1,512,1280]{3,2,1,0:T(8,128)(2,1)S(1)}, bf16[1,1,512,1280]{3,2,1,0:T(8,128)(2,1)}, u32[]{:S(2)}) copy-start(bf16[1,1,512,1280]{3,2,1,0:T(8,128)(2,1)} %param.18) | copy-start | bytes 3932164
  33.8 21.6 %all-to-all-start = ((bf16[8,1,32,1280]{3,2,1,0:T(8,128)(2,1)}), bf16[8,1,32,1280]{3,2,1,0:T(8,128)(2,1)S(1)}, u32[]{:S(2)}, u32[]{:S(2)}) async-start(bf16[8,1,32,1280]{3,2,1,0:T(8,128)(2,1)} %select_select_fusion.1), calls=%async_computation | async-start | bytes 1310720 | tf_op jit(solution)/shard_map/all_to_all | solution.py:198
  55.4 1.4 copy-start.11
  55.4 1.4 copy-start.12
  55.4 1.4 copy-start.17
  56.6 4.5 slice-start
  56.9 4.6 slice-start.1
  56.9 4.6 copy-start.20
  61.5 1.3 copy-start.3
  61.5 1.8 copy-start.6
  61.5 1.8 copy-start.14
  61.5 1.8 copy-start.18
  61.5 1.8 copy-start.21
  63.7 5.5 %copy-start.19 = (s32[1,1,512]{2,1,0:T(1,128)S(1)}, s32[1,1,512]{2,1,0:T(1,128)}, u32[]{:S(2)}) copy-start(s32[1,1,512]{2,1,0:T(1,128)} %param.20) | copy-start | bytes 6148
  63.7 5.5 %copy-start.2 = (bf16[512,512]{1,0:T(8,128)(2,1)S(1)}, bf16[512,512]{1,0:T(8,128)(2,1)}, u32[]{:S(2)}) copy-start(bf16[512,512]{1,0:T(8,128)(2,1)} %param.33) | copy-start | bytes 1572868
  65.7 13.1 %all-to-all-start.1 = ((bf16[8,1,32,512]{3,2,1,0:T(8,128)(2,1)}), bf16[8,1,32,512]{3,2,1,0:T(8,128)(2,1)S(1)}, u32[]{:S(2)}, u32[]{:S(2)}) async-start(bf16[8,1,32,512]{3,2,1,0:T(8,128)(2,1)} %select_select_fusion.4), calls=%async_computation.1 | async-start | bytes 524288 | tf_op jit(solution)/shard_map/all_to_all | solution.py:207
  69.1 172.1 %reduce-scatter.5.cloned.1.call-start = ((), (), s32[]{:S(2)}) async-start(), calls=%async_computation.7 | async-start | bytes 14745600 | tf_op jit(solution)/shard_map/reduce_scatter | solution.py:241
  69.2 2.0 copy-start.15
  78.8 2.0 copy-start.13
  80.8 1.1 copy-start.9
  80.8 1.1 copy-start.16
  100.1 1.3 copy-start.4
  108.0 1.3 copy-start.5
  108.0 268.1 %reduce-scatter.3.cloned.1.call-start = ((), (), s32[]{:S(2)}) async-start(), calls=%async_computation.6 | async-start | bytes 14745600 | tf_op jit(solution)/shard_map/reduce_scatter | solution.py:240
  114.4 0.8 copy-start.7
  122.0 345.2 %all-reduce.4.cloned.1.call-start = ((), (), s32[]{:S(2)}) async-start(), calls=%async_computation.8 | async-start | bytes 6553600 | tf_op jit(solution)/shard_map/psum | solution.py:243
  376.1 1.1 copy-start.8
  383.9 4.6 copy-start.22
  385.0 21.6 %all-to-all-start.3 = ((bf16[8,1,32,1280]{3,2,1,0:T(8,128)(2,1)}), bf16[8,1,32,1280]{3,2,1,0:T(8,128)(2,1)S(1)}, u32[]{:S(2)}, u32[]{:S(2)}) async-start(bf16[8,1,32,1280]{3,2,1,0:T(8,128)(2,1)} %select_select_fusion), calls=%async_computation.3 | async-start | bytes 1310720 | tf_op jit(solution)/shard_map/all_to_all | solution.py:229
  467.3 2.8 copy-start.10
  470.1 1.9 copy-start.1
Sparse Core Ops, SparseCore 0:
  108.2 133.0 reduce-scatter.4
  243.6 132.5 reduce-scatter.2
  379.3 87.9 all-reduce.3
where the time goes:
time: 479 us
  waiting for transfers between devices  353 us (74%)
  matrix products  31.4 us (7%)
  local copies, waits for them, and re-layouts  26.2 us (5%)
  blocking collectives  22.9 us (5%)
  other arithmetic  20.5 us (4%)
  between operations  14.3 us (3%)
  starting transfers between devices  10.6 us (2%)
    reduce_scatter x1, waiting for transfers between devices, shards(): lax.psum_scatter(fc1_term, 'tile', scatter_dimension=0, tiled=True)  135 us
    reduce_scatter x1, waiting for transfers between devices, shards(): lax.psum_scatter(fc2_term, 'tile', scatter_dimension=0, tiled=True)  119 us
    psum x1, waiting for transfers between devices, shards(): totals = lax.psum((shares[0], shares[1]), 'dp')  57.2 us
    all_to_all x1, waiting for transfers between devices, shards(): lax.all_to_all(spread(row_data, send_rows, send_valid, lead_shape), 'tile...  17.7 us
    all_to_all x1, waiting for transfers between devices, shards(): lax.all_to_all(spread(grad_feats, back_rows, back_valid, lead_shape), 'ti...  16.7 us
    all_to_all x1, blocking collectives, shards(): lax.all_to_all(spread(grad_projected, send_rows, send_valid, lead_shape),...  12.3 us
    unnamed x1, blocking collectives  10.6 us
  transfers between devices with their start and end apart: 6, of which 6 were waited for; matrix products, arithmetic and copies ran while one was open for 6% of the time, Pallas kernels for 0%

commit v1 on v0

v1 whole, which is shorter than its diff:
```python
import jax
import jax.numpy as jnp
from jax import lax
from jax.sharding import PartitionSpec as P

epsilon = 1e-06


def layer_norm(values, norm_gain, norm_bias):
    row_mean = jnp.mean(values, axis=-1, keepdims=True)
    centred = values - row_mean
    variance = jnp.mean(centred * centred, axis=-1, keepdims=True)
    inv_std = lax.rsqrt(variance + epsilon)
    scaled = centred * inv_std
    return (scaled * norm_gain + norm_bias, scaled, inv_std)


def norm_back(upstream, scaled, inv_std):
    mean_up = jnp.mean(upstream, axis=-1, keepdims=True)
    mean_cross = jnp.mean(upstream * scaled, axis=-1, keepdims=True)
    return inv_std * (upstream - mean_up - scaled * mean_cross)


def gelu_parts(pre_act):
    normal_cdf = 0.5 * (1.0 + lax.erf(pre_act * 0.7071067811865476))
    density = jnp.exp(-0.5 * pre_act * pre_act) * 0.3989422804014327
    return (pre_act * normal_cdf, normal_cdf + pre_act * density)


def encode(enc_input, enc_params):
    (
        mlp_gain,
        mlp_bias,
        fc1_weight,
        fc1_bias,
        fc2_weight,
        fc2_bias,
        encoder_gain,
        encoder_bias,
        embed_weight,
        embed_bias,
    ) = enc_params
    rows_in = enc_input.astype(jnp.float32)
    mlp_in, mlp_scaled, mlp_inv = layer_norm(rows_in, mlp_gain, mlp_bias)
    mlp_in = mlp_in.astype(jnp.bfloat16)
    pre_act = jnp.dot(mlp_in, fc1_weight, preferred_element_type=jnp.float32) + fc1_bias
    activation, slope = gelu_parts(pre_act)
    hidden = activation.astype(jnp.bfloat16)
    encoded = rows_in + jnp.dot(hidden, fc2_weight, preferred_element_type=jnp.float32) + fc2_bias
    normed, enc_scaled, enc_inv = layer_norm(encoded, encoder_gain, encoder_bias)
    normed = normed.astype(jnp.bfloat16)
    projected = (
        jnp.dot(normed, embed_weight, preferred_element_type=jnp.float32) + embed_bias
    ).astype(jnp.bfloat16)
    saved = (mlp_in, mlp_scaled, mlp_inv, slope, hidden, enc_scaled, enc_inv)
    return (saved, projected)


def encode_back(saved, grad_compact, enc_params):
    (
        mlp_gain,
        mlp_bias,
        fc1_weight,
        fc1_bias,
        fc2_weight,
        fc2_bias,
        encoder_gain,
        encoder_bias,
        embed_weight,
        embed_bias,
    ) = enc_params
    mlp_in, mlp_scaled, mlp_inv, slope, hidden, enc_scaled, enc_inv = saved
    grad_normed = jnp.dot(grad_compact, embed_weight.T, preferred_element_type=jnp.float32)
    grad_encoded = norm_back(grad_normed * encoder_gain, enc_scaled, enc_inv).astype(jnp.bfloat16)
    grad_hidden = jnp.dot(grad_encoded, fc2_weight.T, preferred_element_type=jnp.float32)
    grad_pre = (grad_hidden * slope).astype(jnp.bfloat16)
    grad_mlp_in = jnp.dot(grad_pre, fc1_weight.T, preferred_element_type=jnp.float32)
    grad_feats = (
        grad_encoded.astype(jnp.float32) + norm_back(grad_mlp_in * mlp_gain, mlp_scaled, mlp_inv)
    ).astype(jnp.bfloat16)
    fc1_term = jnp.dot(mlp_in.T, grad_pre, preferred_element_type=jnp.float32)
    fc2_term = jnp.dot(hidden.T, grad_encoded, preferred_element_type=jnp.float32)
    return (fc1_term, fc2_term, grad_feats)


def decoder_pass(
    projected_rows,
    keep_rows,
    position_ids,
    upstream,
    position_table,
    mask_token,
    decoder_gain,
    decoder_bias,
):
    table_ids = jnp.arange(position_table.shape[0], dtype=jnp.int32)[None, :]
    pick = (position_ids[:, None] == table_ids).astype(jnp.bfloat16)
    placed = jnp.dot(pick, position_table, preferred_element_type=jnp.float32)
    dec_input = jnp.where(keep_rows, projected_rows, mask_token) + placed
    decoded, dec_scaled, dec_inv = layer_norm(dec_input, decoder_gain, decoder_bias)
    grad_input = norm_back(upstream.astype(jnp.float32) * decoder_gain, dec_scaled, dec_inv)
    grad_projected = jnp.where(keep_rows, grad_input, 0.0).astype(jnp.bfloat16)
    return (decoded.astype(jnp.bfloat16), grad_projected)


def shards(
    features,
    visible,
    positions,
    cotangent,
    mlp_gain,
    mlp_bias,
    fc1_weight,
    fc1_bias,
    fc2_weight,
    fc2_bias,
    encoder_gain,
    encoder_bias,
    embed_weight,
    embed_bias,
    mask_token,
    position_table,
    decoder_gain,
    decoder_bias,
):
    patch_count = features.shape[2]
    model_width = features.shape[3]
    dec_width = embed_weight.shape[1]
    most_rows = patch_count // 2
    flags = visible.reshape(patch_count)
    row_data = features.reshape(patch_count, model_width)
    keep_rows = (flags > 0)[:, None]
    upstream = cotangent.reshape(patch_count, dec_width)
    ids = jnp.arange(patch_count, dtype=jnp.int32)
    row_rank = jnp.sum(jnp.where(ids[None, :] < ids[:, None], flags[None, :], 0), axis=1)
    slots = jnp.arange(most_rows, dtype=jnp.int32)
    target = jnp.where(flags > 0, row_rank, -1)
    gather = (slots[:, None] == target[None, :]).astype(jnp.bfloat16)
    scatter = (target[:, None] == slots[None, :]).astype(jnp.bfloat16)
    enc_params = (
        mlp_gain,
        mlp_bias,
        fc1_weight,
        fc1_bias,
        fc2_weight,
        fc2_bias,
        encoder_gain,
        encoder_bias,
        embed_weight,
        embed_bias,
    )
    decoder_args = (position_table, mask_token, decoder_gain, decoder_bias)
    enc_input = jnp.dot(gather, row_data, preferred_element_type=jnp.bfloat16)
    saved, projected = encode(enc_input, enc_params)
    projected_rows = jnp.dot(scatter, projected, preferred_element_type=jnp.float32)
    decoded, grad_projected = decoder_pass(
        projected_rows, keep_rows, positions.reshape(-1), upstream, *decoder_args
    )
    grad_compact = jnp.dot(gather, grad_projected, preferred_element_type=jnp.bfloat16)
    fc1_term, fc2_term, grad_feats = encode_back(saved, grad_compact, enc_params)
    grad_rows = jnp.dot(scatter, grad_feats, preferred_element_type=jnp.bfloat16)
    device_total = lax.axis_size("dp") * lax.axis_size("tile")
    totals = []
    for term in (fc1_term, fc2_term):
        share = lax.psum_scatter(
            term.astype(jnp.bfloat16), "tile", scatter_dimension=0, tiled=True
        )
        totals.append(lax.psum(share, "dp").astype(jnp.float32) / device_total)
    fc1_grad, fc2_grad = totals
    feature_grad = grad_rows.reshape(features.shape)
    decoded_out = decoded.reshape(cotangent.shape)
    return (feature_grad, decoded_out, fc1_grad, fc2_grad)


def solution(mesh):
    return jax.shard_map(
        shards,
        mesh=mesh,
        in_specs=(
            P("dp", "tile", None, None),
            P("dp", "tile", None),
            P("dp", "tile", None),
            P("dp", "tile", None, None),
            P(),
            P(),
            P(),
            P(),
            P(),
            P(),
            P(),
            P(),
            P(),
            P(),
            P(),
            P(),
            P(),
            P(),
        ),
        out_specs=(
            P("dp", "tile", None, None),
            P("dp", "tile", None, None),
            P("tile", None),
            P("tile", None),
        ),
        check_vma=False,
    )
```

time: 479 us -> 270 us (0.56)
  waiting for transfers between devices: 353 us -> 195 us
  blocking collectives: 22.9 us -> 0 us
  local copies, waits for them, and re-layouts: 26.2 us -> 7.04 us
  matrix products: 31.4 us -> 41.9 us
  starting transfers between devices: 10.6 us -> 0.3 us
  other arithmetic: 20.5 us -> 10.9 us
    reduce_scatter x2, waiting for transfers between devices: 254 us -> 141 us  [shards(): lax.psum_scatter(term.astype(jnp.bfloat16), 'tile', scatter_dimension=0,...]
    all_to_all x3 -> x0, waiting for transfers between devices: 41.2 us -> none  [the longest x1 17.7 us: shards(): lax.all_to_all(spread(row_data, send_rows, send_valid, lead_shape), 'tile...]
    gather x11 -> x0, local copies, waits for them, and re-layouts: 14.6 us -> none  [the longest x4 4.8 us: spread(): jnp.take(source_rows, indices, axis=0)]
    all_to_all x1 -> x0, blocking collectives: 12.3 us -> none  [shards(): lax.all_to_all(spread(grad_projected, send_rows, send_valid, lead_shape),...]
    unnamed x1 -> x0, blocking collectives: 10.6 us -> none
    all_to_all x3 -> x0, starting transfers between devices: 10.5 us -> none  [the longest x1 3.54 us: shards(): lax.all_to_all(spread(grad_feats, back_rows, back_valid, lead_shape), 'ti...]
    dot_general x1 -> x4, matrix products: 0.4 us -> 8.96 us  [the longest x1 3.22 us: shards(): jnp.dot(scatter, projected, preferred_element_type=jnp.float32)]
    select_n x13 -> x1, other arithmetic: 6.34 us -> 0.69 us  [shards(): target = jnp.where(flags > 0, row_rank, -1)]
  transfers between devices with their start and end apart: 6 -> 3, of which waited for: 6 -> 3; matrix products, arithmetic and copies ran while one was open for 6% -> 6% of each run, Pallas kernels for 0% -> 0%
where the time goes in v1:
time: 270 us
  waiting for transfers between devices  195 us (72%)
  matrix products  41.9 us (16%)
  between operations  14.1 us (5%)
  other arithmetic  10.9 us (4%)
  local copies, waits for them, and re-layouts  7.04 us (3%)
    reduce_scatter x2, waiting for transfers between devices, shards(): lax.psum_scatter(term.astype(jnp.bfloat16), 'tile', scatter_dimension=0,...  141 us
    psum x1, waiting for transfers between devices, shards(): totals.append(lax.psum(share, 'dp').astype(jnp.float32) / device_total)  54.3 us
    unnamed x44, local copies, waits for them, and re-layouts  7.04 us
    dot_general x1, matrix products, encode_back(): jnp.dot(hidden.T, grad_encoded, preferred_element_type=jnp.float32)  6.71 us
  transfers between devices with their start and end apart: 3, of which 3 were waited for; matrix products, arithmetic and copies ran while one was open for 6% of the time, Pallas kernels for 0%

profile of v1, /device:TPU:0, one launch (start us, length us, event | category | flops | bytes accessed | tf_op | source)
XLA Modules:
  0.0 269.7 jit_solution(12920631367889845395)
XLA Ops:
  7.2 0.9 select_reduce_fusion
  8.1 0.7 broadcast_select_fusion
  8.8 1.9 fusion.60
  10.8 0.3 multiply_reduce_fusion.3
  11.1 0.4 copy-done.8
  11.5 5.2 %convolution_add_fusion = f32[256,2560]{1,0:T(8,128)S(1)} fusion(bf16[1280,2560]{1,0:T(8,128)(2,1)} %param.24, f32[2560]{0:T(1024)S(1)} %copy-done.13, f32[256,1280]{1,0:T(8,128)S(1)} %get-tuple-element.24, f32[1280]{0:T(1024)S(1)} %copy-done.8, f32[1280]{0:T(1024)S(1)} %copy-done.9, f32[256]{0:T(256)S(1)} %add_rsqrt_fusion.2, ...), kind=kOutput, calls=%fused_computation.3 | convolution fusion | flops 1680015360 | bytes 10508288 | tf_op jit(solution)/shard_map/dot_general | solution.py:46
  16.7 2.2 fusion.61
  19.0 1.0 copy-done.4
  20.0 0.3 multiply_reduce_fusion.2
  20.3 3.2 %convolution_select_fusion = f32[512,512]{0,1:T(8,128)} fusion(bf16[1280,512]{1,0:T(8,128)(2,1)S(1)} %copy-done, f32[256,1280]{1,0:T(8,128)} %copy-done.4, f32[1280]{0:T(1024)S(1)} %copy-done.15, f32[1280]{0:T(1024)S(1)} %copy-done.16, f32[256]{0:T(256)S(1)} %add_rsqrt_fusion.1, f32[256]{0:T(256)S(1)} %broadcast_multiply_fusion.7, f32[512]{0:T(512)S(1)} %copy-done.17, ...), kind=kOutput, calls=%fused_computation.21 | convolution fusion | flops 472055808 | bytes 3688960 | tf_op jit(solution)/shard_map/dot_general | solution.py:155
  23.6 1.9 fusion.62
  25.5 0.9 copy-done.1
  26.4 0.2 multiply_reduce_fusion.4
  26.6 1.3 copy.24
  27.9 2.4 fusion.12
  30.3 3.7 %fusion.59 = (f32[256]{0:T(256)S(1)}, f32[256]{0:T(256)S(1)}, f32[256,1280]{1,0:T(8,128)}) fusion(f32[256]{0:T(256)S(1)} %add_rsqrt_fusion.1, f32[256,1280]{1,0:T(8,128)} %copy-done.4, f32[256]{0:T(256)S(1)} %broadcast_multiply_fusion.7, f32[1280]{0:T(1024)S(1)} %copy-done.16, bf16[1280,512]{1,0:T(8,128)(2,1)S(1)} %copy-done, f32[512,512]{0,1:T(8,128)} %copy-done.1, ...), kind=kOutput, calls=%fused_computation.92 | convolution fusion | flops 474480128 | bytes 5527040 | tf_op jit(solution)/shard_map/dot_general | solution.py:73
  34.1 2.2 multiply_convert_fusion.1
  36.3 0.3 copy-done.3
  36.6 5.0 %fusion = bf16[256,2560]{1,0:T(8,128)(2,1)S(1)} fusion(bf16[256,1280]{1,0:T(8,128)(2,1)S(1)} %multiply_convert_fusion.1, bf16[2560,1280]{1,0:T(8,128)(2,1)} %param.26, f32[256,2560]{1,0:T(8,128)S(1)} %copy-done.3), kind=kOutput, calls=%fused_computation.5 | convolution fusion | flops 1684275200 | bytes 11141120 | tf_op jit(solution)/shard_map/dot_general | solution.py:75
  41.7 1.0 copy-done.5
  42.7 4.8 %convolution_convert_fusion.1 = bf16[1280,2560]{1,0:T(8,128)(2,1)} fusion(bf16[256,2560]{1,0:T(8,128)(2,1)S(1)} %fusion, f32[256,1280]{1,0:T(8,128)S(1)} %get-tuple-element.24, f32[1280]{0:T(1024)S(1)} %copy-done.8, f32[1280]{0:T(1024)S(1)} %copy-done.9, f32[256]{0:T(256)S(1)} %add_rsqrt_fusion.2, f32[256]{0:T(256)S(1)} %broadcast_multiply_fusion.8), kind=kOutput, calls=%fused_computation.1 | convolution fusion | flops 1682636800 | bytes 9187328 | tf_op jit(solution)/shard_map/dot_general | solution.py:81
  47.5 0.2 reduce-scatter.5.cloned.1.call-start
  47.7 6.7 %convolution_convert_fusion = bf16[2560,1280]{1,0:T(8,128)(2,1)} fusion(bf16[256,1280]{1,0:T(8,128)(2,1)S(1)} %multiply_convert_fusion.1, f32[256,2560]{1,0:T(8,128)} %copy-done.2), kind=kOutput, calls=%fused_computation | convolution fusion | flops 1684275200 | bytes 9830400 | tf_op jit(solution)/shard_map/dot_general | solution.py:82
  54.5 0.0 all-reduce.3.cloned.1.call-start
  54.5 68.1 %reduce-scatter.3.cloned.1.call-done = bf16[160,2560]{1,0:T(8,128)(2,1)} async-done(((bf16[1280,2560]{1,0:T(8,128)(2,1)}), bf16[160,2560]{1,0:T(8,128)(2,1)}) %reduce-scatter.3.cloned.1.call-update) | async-done | bytes 819216 | tf_op jit(solution)/shard_map/reduce_scatter | solution.py:165
  122.6 73.0 %reduce-scatter.5.cloned.1.call-done = bf16[320,1280]{1,0:T(8,128)(2,1)} async-done(((bf16[2560,1280]{1,0:T(8,128)(2,1)}), bf16[320,1280]{1,0:T(8,128)(2,1)}) %reduce-scatter.5.cloned.1.call-update) | async-done | bytes 819216 | tf_op jit(solution)/shard_map/reduce_scatter | solution.py:165
  195.6 2.0 copy.25
  197.7 5.3 %fusion.58 = (f32[256]{0:T(256)S(1)}, f32[256]{0:T(256)S(1)}, f32[256,1280]{1,0:T(8,128)S(1)}) fusion(f32[256]{0:T(256)S(1)} %add_rsqrt_fusion.2, f32[256,1280]{1,0:T(8,128)S(1)} %get-tuple-element.24, f32[256]{0:T(256)S(1)} %broadcast_multiply_fusion.8, f32[1280]{0:T(1024)S(1)} %copy-done.9, bf16[256,2560]{1,0:T(8,128)(2,1)} %copy-done.5, ...), kind=kOutput, calls=%fused_computation.91 | convolution fusion | flops 1679687168 | bytes 10494976 | tf_op jit(solution)/shard_map/dot_general | solution.py:77
  203.0 2.0 convolution_bitcast_fusion
  205.0 54.3 %all-reduce.3.cloned.1.call-done = (bf16[160,2560]{1,0:T(8,128)(2,1)}, bf16[320,1280]{1,0:T(8,128)(2,1)}) async-done(((bf16[160,2560]{1,0:T(8,128)(2,1)}, bf16[320,1280]{1,0:T(8,128)(2,1)}), (bf16[160,2560]{1,0:T(8,128)(2,1)}, bf16[320,1280]{1,0:T(8,128)(2,1)})) %all-reduce.3.cloned.1.call-update) | async-done | bytes 1638416 | tf_op jit(solution)/shard_map/psum | solution.py:168
  259.3 2.5 convert_multiply_fusion
  261.8 1.3 convert_multiply_fusion.1
  (53 shorter events, 0.3 us)
Async XLA Ops:
  7.2 13.1 %copy-start = (bf16[1280,512]{1,0:T(8,128)(2,1)S(1)}, bf16[1280,512]{1,0:T(8,128)(2,1)}, u32[]{:S(2)}) copy-start(bf16[1280,512]{1,0:T(8,128)(2,1)} %param.30) | copy-start | bytes 3932164
  7.2 115.5 %reduce-scatter.3.cloned.1.call-start = ((), (), s32[]{:S(2)}) async-start(), calls=%async_computation.2 | async-start | bytes 7372800 | tf_op jit(solution)/shard_map/reduce_scatter | solution.py:165
  10.7 0.7 copy-start.8
  10.8 0.7 copy-start.9
  10.8 0.7 copy-start.13
  10.8 5.9 %slice-start = ((s8[6553600]{0:T(1024)(128)(4,1)}), s8[4194304]{0:T(1024)(128)(4,1)S(1)}, s32[]{:S(2)}) async-start(s8[6553600]{0:T(1024)(128)(4,1)} %bitcast.36), calls=%async_computation.5 | async-start | bytes 8388608
  11.5 5.2 %slice-start.1 = ((s8[6553600]{0:T(1024)(128)(4,1)}), s8[2359296]{0:T(1024)(128)(4,1)S(1)}, s32[]{:S(2)}) async-start(s8[6553600]{0:T(1024)(128)(4,1)} %bitcast.36), calls=%async_computation.6 | async-start | bytes 4718592
  11.5 5.2 %copy-start.14 = (f32[1280]{0:T(1024)S(1)}, f32[1280]{0:T(1024)}, u32[]{:S(2)}) copy-start(f32[1280]{0:T(1024)} %param.27) | copy-start | bytes 15364
  16.7 2.2 copy-start.2
  18.9 1.1 copy-start.4
  18.9 1.3 copy-start.15
  18.9 1.3 copy-start.16
  19.0 1.3 copy-start.17
  19.0 1.3 copy-start.18
  20.3 3.3 %copy-start.7 = (bf16[512,512]{1,0:T(8,128)(2,1)S(1)}, bf16[512,512]{1,0:T(8,128)(2,1)}, u32[]{:S(2)}) copy-start(bf16[512,512]{1,0:T(8,128)(2,1)} %param.33) | copy-start | bytes 1572868
  20.3 3.2 %copy-start.10 = (s32[1,1,512]{2,1,0:T(1,128)S(1)}, s32[1,1,512]{2,1,0:T(1,128)}, u32[]{:S(2)}) copy-start(s32[1,1,512]{2,1,0:T(1,128)} %param.20) | copy-start | bytes 6148
  25.5 1.0 copy-start.1
  25.5 2.4 copy-start.11
  25.5 2.4 copy-start.12
  34.1 2.5 copy-start.3
  41.6 1.1 copy-start.5
  47.5 148.1 %reduce-scatter.5.cloned.1.call-start = ((), (), s32[]{:S(2)}) async-start(), calls=%async_computation.3 | async-start | bytes 7372800 | tf_op jit(solution)/shard_map/reduce_scatter | solution.py:165
  54.5 204.9 %all-reduce.3.cloned.1.call-start = ((), (), s32[]{:S(2)}) async-start(), calls=%async_computation.4 | async-start | bytes 3276800 | tf_op jit(solution)/shard_map/psum | solution.py:168
  259.3 2.5 copy-start.6
Sparse Core Ops, SparseCore 0:
  47.6 74.9 reduce-scatter.2
  125.0 70.6 reduce-scatter.4
  198.8 60.5 all-reduce.2

commit v2 on v1

--- a/solution.py
+++ b/solution.py
@@ -1,7 +1,13 @@
+import functools
+
 import jax
 import jax.numpy as jnp
 from jax import lax
+from jax.experimental import pallas as pl
+from jax.experimental.pallas import tpu as pltpu
 from jax.sharding import PartitionSpec as P
+
+MESH = pl.DeviceIdType.MESH
 
 epsilon = 1e-06
 
@@ -78,9 +84,7 @@
     grad_feats = (
         grad_encoded.astype(jnp.float32) + norm_back(grad_mlp_in * mlp_gain, mlp_scaled, mlp_inv)
     ).astype(jnp.bfloat16)
-    fc1_term = jnp.dot(mlp_in.T, grad_pre, preferred_element_type=jnp.float32)
-    fc2_term = jnp.dot(hidden.T, grad_encoded, preferred_element_type=jnp.float32)
-    return (fc1_term, fc2_term, grad_feats)
+    return (mlp_in, grad_pre, hidden, grad_encoded, grad_feats)
 
 
 def decoder_pass(
@@ -101,6 +105,250 @@
     grad_input = norm_back(upstream.astype(jnp.float32) * decoder_gain, dec_scaled, dec_inv)
     grad_projected = jnp.where(keep_rows, grad_input, 0.0).astype(jnp.bfloat16)
     return (decoded.astype(jnp.bfloat16), grad_projected)
+
+
+def reduce_kernel(
+    chunks,
+    z_count,
+    lhs_a,
+    rhs_a,
+    lhs_b,
+    rhs_b,
+    out_a,
+    out_b,
+    acc_a,
+    acc_b,
+    send0_a,
+    send0_b,
+    land0_a,
+    land0_b,
+    send1_a,
+    send1_b,
+    land1_a,
+    land1_b,
+    send2_a,
+    send2_b,
+    land2_a,
+    land2_b,
+    send3_a,
+    send3_b,
+    land3_a,
+    land3_b,
+    pair_sems,
+    z_sems,
+    spread_sems,
+):
+    dp = lax.axis_index("dp")
+    tile = lax.axis_index("tile")
+    x = lax.rem(dp, 2)
+    y = lax.div(dp, 2)
+    core = lax.rem(tile, 2)
+    my_z = lax.div(tile, 2)
+    sibling = (dp, tile + 1 - 2 * core)
+    across_x = (dp + 1 - 2 * x, tile)
+    across_y = (dp + 2 - 4 * y, tile)
+    diagonal = (3 - dp, tile)
+    z_to = [lax.rem(my_z + k, z_count) for k in range(1, z_count)]
+    peers = [sibling, across_x, across_y, diagonal]
+    peers += [(dp, 2 * z + core) for z in z_to]
+
+    barrier = pltpu.get_barrier_semaphore()
+    for peer in peers:
+        pl.semaphore_signal(barrier, inc=1, device_id=peer, device_id_type=MESH)
+    pl.semaphore_wait(barrier, len(peers))
+
+    tensors = (
+        (lhs_a, rhs_a, out_a, acc_a, send0_a, land0_a, send1_a, land1_a, send2_a, land2_a,
+         send3_a, land3_a, x, y, across_x, across_y),
+        (lhs_b, rhs_b, out_b, acc_b, send0_b, land0_b, send1_b, land1_b, send2_b, land2_b,
+         send3_b, land3_b, y, x, across_y, across_x),
+    )
+    copies = {}
+
+    def send(key, src, dst, sems, at, peer):
+        copy = pltpu.make_async_remote_copy(
+            src_ref=src,
+            dst_ref=dst,
+            send_sem=sems.at[(0,) + at],
+            recv_sem=sems.at[(1,) + at],
+            device_id=peer,
+            device_id_type=MESH,
+        )
+        copy.start()
+        copies[key] = copy
+
+    def products(t, j, which, store):
+        lhs, rhs = tensors[t][0], tensors[t][1]
+        if t == 0:
+            m = lhs.shape[2] // z_count
+
+            @pl.loop(0, 4)
+            def _(e):
+                part = jnp.dot(lhs[j, which], rhs[e], preferred_element_type=jnp.float32)
+                for z in range(z_count):
+                    store(lax.div(e, 2), lax.rem(e, 2), z, part[z * m : (z + 1) * m])
+        else:
+            m = lhs.shape[3] // z_count
+
+            @pl.loop(0, 4)
+            def _(e):
+                part = jnp.dot(lhs[j, which, e], rhs[...], preferred_element_type=jnp.float32)
+                for z in range(z_count):
+                    store(lax.div(e, 2), lax.rem(e, 2), z, part[z * m : (z + 1) * m])
+
+    def stage0(t, j):
+        acc, send0, land0 = tensors[t][3:6]
+
+        def store_send(f, g, z, value):
+            send0[j, f, g, z] = value.astype(jnp.bfloat16)
+
+        def store_own(f, g, z, value):
+            acc[j, f, g, z] = value
+
+        products(t, j, 1 - core, store_send)
+        send(("c", t, j), send0.at[j], land0.at[j], pair_sems, (0, t, j), sibling)
+        products(t, j, core, store_own)
+
+    def stage1(t, j):
+        acc, _, land0, send1, land1 = tensors[t][3:8]
+        f, partner = tensors[t][12], tensors[t][14]
+        copies["c", t, j].wait()
+
+        @pl.loop(0, z_count)
+        def _(z):
+            for g in range(2):
+                send1[j, g, z] = (
+                    acc[j, 1 - f, g, z] + land0[j, 1 - f, g, z].astype(jnp.float32)
+                ).astype(jnp.bfloat16)
+
+        send(("f", t, j), send1.at[j], land1.at[j], pair_sems, (1, t, j), partner)
+
+        @pl.loop(0, z_count)
+        def _(z):
+            for g in range(2):
+                acc[j, f, g, z] = acc[j, f, g, z] + land0[j, f, g, z].astype(jnp.float32)
+
+    def stage2(t, j):
+        acc = tensors[t][3]
+        land1, send2, land2 = tensors[t][7:10]
+        f, g, partner = tensors[t][12], tensors[t][13], tensors[t][15]
+        copies["f", t, j].wait()
+
+        @pl.loop(0, z_count)
+        def _(z):
+            send2[j, z] = (
+                acc[j, f, 1 - g, z] + land1[j, 1 - g, z].astype(jnp.float32)
+            ).astype(jnp.bfloat16)
+
+        send(("g", t, j), send2.at[j], land2.at[j], pair_sems, (2, t, j), partner)
+
+        @pl.loop(0, z_count)
+        def _(z):
+            acc[j, f, g, z] = acc[j, f, g, z] + land1[j, g, z].astype(jnp.float32)
+
+    def stage3(t, j):
+        acc = tensors[t][3]
+        land2, send3, land3 = tensors[t][9:12]
+        f, g = tensors[t][12], tensors[t][13]
+        copies["g", t, j].wait()
+        for k, z in enumerate(z_to):
+            send3[j, k] = (acc[j, f, g, z] + land2[j, z].astype(jnp.float32)).astype(jnp.bfloat16)
+            send(
+                ("z", t, j, k), send3.at[j, k], land3.at[j, k], z_sems, (t, j, k),
+                (dp, 2 * z + core),
+            )
+        acc[j, f, g, my_z] = acc[j, f, g, my_z] + land2[j, my_z].astype(jnp.float32)
+
+    def stage4(t, j):
+        out, acc = tensors[t][2:4]
+        land3 = tensors[t][11]
+        f, g = tensors[t][12], tensors[t][13]
+        total = acc[j, f, g, my_z]
+        for k in range(z_count - 1):
+            copies["z", t, j, k].wait()
+            total = total + land3[j, k].astype(jnp.float32)
+        mine = 2 * f + g
+        out[mine, j] = total.astype(jnp.bfloat16)
+        for k, peer in enumerate((across_x, across_y, diagonal)):
+            send(
+                ("s", t, j, k), out.at[mine, j], out.at[mine, j], spread_sems, (t, j, k), peer
+            )
+
+    stages = (stage0, stage1, stage2, stage3, stage4)
+    for step in range(chunks + len(stages) - 1):
+        for at in reversed(range(len(stages))):
+            j = step - at
+            if 0 <= j < chunks:
+                for t in range(2):
+                    stages[at](t, j)
+    for j in range(chunks):
+        for t in range(2):
+            for k in range(3):
+                copies["s", t, j, k].wait()
+
+
+def reduce_weights(mlp_in, grad_pre, hidden, grad_encoded, tiles):
+    rows, width = mlp_in.shape
+    inner = hidden.shape[1]
+    z_count = tiles // 2
+    rows_a, rows_b = width // tiles, inner // tiles // 4
+    chunks = 5
+    m_a, n_a = rows_a // chunks, inner // 4
+    m_b, n_b = rows_b // chunks, width
+    lhs_a = mlp_in.T.reshape(z_count, 2, chunks, m_a, rows).transpose(2, 1, 0, 3, 4)
+    lhs_a = lhs_a.reshape(chunks, 2, z_count * m_a, rows)
+    rhs_a = grad_pre.reshape(rows, 4, n_a).transpose(1, 0, 2)
+    lhs_b = hidden.T.reshape(z_count, 2, 4, chunks, m_b, rows).transpose(3, 1, 2, 0, 4, 5)
+    lhs_b = lhs_b.reshape(chunks, 2, 4, z_count * m_b, rows)
+    whole = pl.BlockSpec(memory_space=pltpu.VMEM)
+    half, full = jnp.bfloat16, jnp.float32
+    scratch = []
+    for lead, kind in (
+        ((2, 2, z_count), full),
+        ((2, 2, z_count), half),
+        ((2, 2, z_count), half),
+        ((2, z_count), half),
+        ((2, z_count), half),
+        ((z_count,), half),
+        ((z_count,), half),
+        ((z_count - 1,), half),
+        ((z_count - 1,), half),
+    ):
+        for m, n in ((m_a, n_a), (m_b, n_b)):
+            scratch.append(pltpu.VMEM((chunks,) + lead + (m, n), kind))
+    scratch += [
+        pltpu.SemaphoreType.DMA((2, 3, 2, chunks)),
+        pltpu.SemaphoreType.DMA((2, 2, chunks, z_count - 1)),
+        pltpu.SemaphoreType.DMA((2, 2, chunks, 3)),
+    ]
+    out_a, out_b = pl.pallas_call(
+        functools.partial(reduce_kernel, chunks, z_count),
+        out_shape=(
+            jax.ShapeDtypeStruct((4, chunks, m_a, n_a), half),
+            jax.ShapeDtypeStruct((4, chunks, m_b, n_b), half),
+        ),
+        in_specs=[whole] * 4,
+        out_specs=(whole, whole),
+        scratch_shapes=scratch,
+        compiler_params=pltpu.CompilerParams(
+            collective_id=0, has_side_effects=True, vmem_limit_bytes=56 * 2**20
+        ),
+    )(lhs_a, rhs_a, lhs_b, grad_encoded)
+    fc1 = out_a.reshape(4, rows_a, n_a).transpose(1, 0, 2).reshape(rows_a, inner)
+    fc2 = out_b.reshape(4 * rows_b, n_b)
+    return fc1.astype(full), fc2.astype(full)
+
+
+def reducible(mlp_in, hidden, scenes, tiles):
+    width, inner = mlp_in.shape[1], hidden.shape[1]
+    return (
+        scenes == 4
+        and tiles % 2 == 0
+        and width % (tiles * 5 * 16) == 0
+        and inner % (tiles * 4 * 5 * 16) == 0
+        and inner % (4 * 128) == 0
+        and width % 128 == 0
+    )
 
 
 def shards(
@@ -157,16 +405,23 @@
         projected_rows, keep_rows, positions.reshape(-1), upstream, *decoder_args
     )
     grad_compact = jnp.dot(gather, grad_projected, preferred_element_type=jnp.bfloat16)
-    fc1_term, fc2_term, grad_feats = encode_back(saved, grad_compact, enc_params)
+    mlp_in, grad_pre, hidden, grad_encoded, grad_feats = encode_back(
+        saved, grad_compact, enc_params
+    )
     grad_rows = jnp.dot(scatter, grad_feats, preferred_element_type=jnp.bfloat16)
     device_total = lax.axis_size("dp") * lax.axis_size("tile")
-    totals = []
-    for term in (fc1_term, fc2_term):
-        share = lax.psum_scatter(
-            term.astype(jnp.bfloat16), "tile", scatter_dimension=0, tiled=True
-        )
-        totals.append(lax.psum(share, "dp").astype(jnp.float32) / device_total)
-    fc1_grad, fc2_grad = totals
+    tiles = lax.axis_size("tile")
+    if reducible(mlp_in, hidden, lax.axis_size("dp"), tiles):
+        totals = reduce_weights(mlp_in, grad_pre, hidden, grad_encoded, tiles)
+    else:
+        totals = []
+        for left, right in ((mlp_in, grad_pre), (hidden, grad_encoded)):
+            term = jnp.dot(left.T, right, preferred_element_type=jnp.float32)
+            share = lax.psum_scatter(
+                term.astype(jnp.bfloat16), "tile", scatter_dimension=0, tiled=True
+            )
+            totals.append(lax.psum(share, "dp").astype(jnp.float32))
+    fc1_grad, fc2_grad = [total / device_total for total in totals]
     feature_grad = grad_rows.reshape(features.shape)
     decoded_out = decoded.reshape(cotangent.shape)
     return (feature_grad, decoded_out, fc1_grad, fc2_grad)

time: 270 us -> 162 us (0.60)
  waiting for transfers between devices: 195 us -> 0 us
  Pallas kernels: 0 us -> 93.4 us
  between operations: 14.1 us -> 0.88 us
  local copies, waits for them, and re-layouts: 7.04 us -> 18.5 us
  matrix products: 41.9 us -> 37.9 us
    reduce_scatter x2 -> x0, waiting for transfers between devices: 141 us -> none  [shards(): lax.psum_scatter(term.astype(jnp.bfloat16), 'tile', scatter_dimension=0,...]
    pallas_call x0 -> x1, Pallas kernels: none -> 93.4 us  [reduce_weights(): pl.pallas_call(functools.partial(reduce_kernel, chunks, z_count), out_sha...]
    psum x1 -> x0, waiting for transfers between devices: 54.3 us -> none  [shards(): totals.append(lax.psum(share, 'dp').astype(jnp.float32) / device_total)]
    dot_general x2 -> x0, matrix products: 11.5 us -> none  [the longest x1 6.71 us: encode_back(): jnp.dot(hidden.T, grad_encoded, preferred_element_type=jnp.float32)]
    convert_element_type x0 -> x3, local copies, waits for them, and re-layouts: none -> 6.15 us  [the longest x1 2.42 us: encode(): hidden = activation.astype(jnp.bfloat16)]
    dot_general x1, matrix products: 2.2 us -> 5.74 us  [encode(): jnp.dot(hidden, fc2_weight, preferred_element_type=jnp.float32)]
    transpose x0 -> x2, local copies, waits for them, and re-layouts: none -> 3.47 us  [the longest x1 2.57 us: reduce_weights(): hidden.T.reshape(z_count, 2, 4, chunks, m_b, rows)]
    unnamed x44 -> x38, local copies, waits for them, and re-layouts: 7.04 us -> 5.06 us
  transfers between devices with their start and end apart: 3 -> 0, of which waited for: 3 -> 0; matrix products, arithmetic and copies ran while one was open for 6% -> 0% of each run, Pallas kernels for 0% -> 0%
where the time goes in v2:
time: 162 us
  Pallas kernels  93.4 us (58%)
  matrix products  37.9 us (23%)
  local copies, waits for them, and re-layouts  18.5 us (11%)
  other arithmetic  11.1 us (7%)
    pallas_call x1, Pallas kernels, reduce_weights(): pl.pallas_call(functools.partial(reduce_kernel, chunks, z_count), out_sha...  93.4 us
    dot_general x1, matrix products, encode(): jnp.dot(mlp_in, fc1_weight, preferred_element_type=jnp.float32) + fc1_bias  6.82 us
    dot_general x1, matrix products, encode_back(): jnp.dot(grad_encoded, fc2_weight.T, preferred_element_type=jnp.float32)  6.32 us
    dot_general x1, matrix products, encode_back(): jnp.dot(grad_pre, fc1_weight.T, preferred_element_type=jnp.float32)  6.21 us
    dot_general x1, matrix products, encode(): jnp.dot(hidden, fc2_weight, preferred_element_type=jnp.float32)  5.74 us
    unnamed x38, local copies, waits for them, and re-layouts  5.06 us
    reduce_sum x2, other arithmetic, norm_back(): mean_up = jnp.mean(upstream, axis=-1, keepdims=True)  3.8 us
    dot_general x1, matrix products, encode_back(): jnp.dot(grad_compact, embed_weight.T, preferred_element_type=jnp.float32)  3.75 us

profile of v2, /device:TPU:0, one launch (start us, length us, event | category | flops | bytes accessed | tf_op | source)
XLA Modules:
  0.0 161.7 jit_solution(9476769990361755659)
XLA Ops:
  0.6 0.9 select_reduce_fusion
  1.6 0.7 broadcast_select_fusion
  2.3 1.3 copy.36
  3.5 1.9 %fusion.65 = (f32[256]{0:T(256)S(1)}, f32[256,1280]{1,0:T(8,128)S(1)}) fusion(bf16[1,1,512,1280]{3,2,1,0:T(8,128)(2,1)} %param.18, s32[512]{0:T(512)S(1)} %get-tuple-element.26), kind=kOutput, calls=%fused_computation.98 | convolution fusion | flops 336330496 | bytes 2624512 | tf_op jit(solution)/shard_map/dot_general | solution.py:401
  5.5 0.3 multiply_reduce_fusion.3
  5.8 0.4 copy-done.6
  6.2 6.8 %fusion.9 = (bf16[2560,256]{0,1:T(8,128)(2,1)}, f32[256,2560]{1,0:T(8,128)}) fusion(f32[2560]{0:T(1024)S(1)} %copy-done.11, bf16[1280,2560]{1,0:T(8,128)(2,1)} %param.24, f32[256,1280]{1,0:T(8,128)S(1)} %get-tuple-element.31, f32[1280]{0:T(1024)S(1)} %copy-done.6, f32[1280]{0:T(1024)S(1)} %copy-done.7, f32[256]{0:T(256)S(1)} %add_rsqrt_fusion.2, ...), kind=kOutput, calls=%fused_computation.20 | convolution fusion | flops 1683292160 | bytes 11819008 | tf_op jit(solution)/shard_map/dot_general | solution.py:52
  13.0 2.4 %copy.41 = bf16[2560,256]{1,0:T(8,128)(2,1)} copy(bf16[2560,256]{0,1:T(8,128)(2,1)} %get-tuple-element.37) | data formatting | bytes 2621440 | tf_op jit(solution)/shard_map/convert_element_type | solution.py:54
  15.4 2.6 %copy.42 = bf16[5,2,4,4,16,256]{5,4,3,2,1,0:T(8,128)(2,1)} copy(bf16[5,2,4,4,16,256]{5,4,0,2,1,3:T(8,128)(2,1)} %bitcast.63) | data formatting | bytes 2621440 | tf_op jit(solution)/shard_map/transpose | solution.py:301
  18.0 5.7 %fusion.66 = (f32[256]{0:T(256)S(1)}, f32[256,1280]{1,0:T(8,128)S(1)}) fusion(f32[1280]{0:T(1024)S(1)} %copy-done.12, f32[256,1280]{1,0:T(8,128)S(1)} %get-tuple-element.31, bf16[2560,1280]{1,0:T(8,128)(2,1)} %param.26, f32[256,2560]{1,0:T(8,128)} %get-tuple-element.38), kind=kOutput, calls=%fused_computation.99 | convolution fusion | flops 1681981184 | bytes 11802624 | tf_op jit(solution)/shard_map/dot_general | solution.py:55
  23.8 1.0 copy-done.4
  24.8 0.3 multiply_reduce_fusion.2
  25.1 3.2 %convolution_select_fusion = f32[512,512]{0,1:T(8,128)} fusion(bf16[1280,512]{1,0:T(8,128)(2,1)S(1)} %copy-done, f32[256,1280]{1,0:T(8,128)} %copy-done.4, f32[1280]{0:T(1024)S(1)} %copy-done.13, f32[1280]{0:T(1024)S(1)} %copy-done.14, f32[256]{0:T(256)S(1)} %add_rsqrt_fusion.1, f32[256]{0:T(256)S(1)} %broadcast_multiply_fusion.7, f32[512]{0:T(512)S(1)} %copy-done.15, ...), kind=kOutput, calls=%fused_computation.25 | convolution fusion | flops 472055808 | bytes 3688960 | tf_op jit(solution)/shard_map/dot_general | solution.py:403
  28.3 2.1 %fusion.67 = (f32[512]{0:T(512)S(1)}, f32[512,512]{0,1:T(8,128)S(1)}) fusion(f32[512,512]{0,1:T(8,128)} %convolution_select_fusion, bf16[512,512]{1,0:T(8,128)(2,1)} %param.33, s32[512]{0:T(512)S(1)} %bitcast.73), kind=kOutput, calls=%fused_computation.100 | convolution fusion | flops 269221376 | bytes 2625536 | tf_op jit(solution)/shard_map/dot_general | solution.py:102
  30.4 0.2 multiply_reduce_fusion.4
  30.6 1.2 fusion.16
  31.8 3.7 %fusion.64 = (f32[256]{0:T(256)S(1)}, f32[256]{0:T(256)S(1)}, f32[256,1280]{1,0:T(8,128)}) fusion(f32[256]{0:T(256)S(1)} %add_rsqrt_fusion.1, f32[256,1280]{1,0:T(8,128)} %copy-done.4, f32[256]{0:T(256)S(1)} %broadcast_multiply_fusion.7, f32[1280]{0:T(1024)S(1)} %copy-done.14, bf16[1280,512]{1,0:T(8,128)(2,1)S(1)} %copy-done, f32[512,512]{0,1:T(8,128)} %copy-done.1, ...), kind=kOutput, calls=%fused_computation.97 | convolution fusion | flops 474480128 | bytes 5527040 | tf_op jit(solution)/shard_map/dot_general | solution.py:79
  35.6 2.2 %multiply_convert_fusion.2.rhs_b = bf16[256,1280]{1,0:T(8,128)(2,1)S(1)} fusion(f32[256,1280]{1,0:T(8,128)} %get-tuple-element.36, f32[256,1280]{1,0:T(8,128)} %copy-done.4, f32[256]{0:T(256)S(1)} %broadcast_multiply_fusion.5, f32[256]{0:T(256)S(1)} %broadcast_multiply_fusion.6, f32[256]{0:T(256)S(1)} %add_rsqrt_fusion.1, f32[256]{0:T(256)S(1)} %broadcast_multiply_fusion.7), kind=kLoop, calls=%fused_computation.29 | loop fusion | flops 2293760 | bytes 3280896 | tf_op jit(solution)/shard_map/convert_element_type | solution.py:80
  37.8 0.3 copy-done.17
  38.1 6.3 %fusion = bf16[256,2560]{1,0:T(8,128)(2,1)} fusion(bf16[256,1280]{1,0:T(8,128)(2,1)S(1)} %multiply_convert_fusion.2.rhs_b, bf16[2560,1280]{1,0:T(8,128)(2,1)} %param.26, f32[256,2560]{1,0:T(8,128)S(1)} %copy-done.17), kind=kOutput, calls=%fused_computation.3 | convolution fusion | flops 1684275200 | bytes 11141120 | tf_op jit(solution)/shard_map/dot_general | solution.py:81
  44.4 2.0 %copy.44 = bf16[1,1,512,512]{3,2,1,0:T(8,128)(2,1)} copy(bf16[1,1,512,512]{2,3,1,0:T(8,128)(2,1)} %get-tuple-element.29) | data formatting | bytes 1048576
  46.4 6.2 %convolution_multiply_fusion.1 = f32[256,1280]{1,0:T(8,128)} fusion(bf16[256,2560]{1,0:T(8,128)(2,1)} %fusion, bf16[1280,2560]{1,0:T(8,128)(2,1)} %param.24, f32[1280]{0:T(1024)S(1)} %copy-done.7), kind=kOutput, calls=%fused_computation.4 | convolution fusion | flops 1678049280 | bytes 9180160 | tf_op jit(solution)/shard_map/dot_general | solution.py:83
  52.7 2.4 %copy.39 = bf16[256,2560]{0,1:T(8,128)(2,1)} copy(bf16[256,2560]{1,0:T(8,128)(2,1)} %fusion) | data formatting | bytes 2621440 | tf_op jit(solution)/shard_map/convert_element_type | solution.py:82
  55.1 2.4 %copy.40 = bf16[256,4,640]{2,0,1:T(8,128)(2,1)} copy(bf16[256,4,640]{0,2,1:T(8,128)(2,1)} %bitcast.64) | data formatting | bytes 2621440 | tf_op jit(solution)/shard_map/reshape | solution.py:300
  57.5 2.6 %fusion.63 = (f32[256]{0:T(256)S(1)}, f32[256]{0:T(256)S(1)}, bf16[1280,256]{0,1:T(8,128)(2,1)}) fusion(f32[256,1280]{1,0:T(8,128)} %convolution_multiply_fusion.1, f32[256]{0:T(256)S(1)} %add_rsqrt_fusion.2, f32[256,1280]{1,0:T(8,128)S(1)} %get-tuple-element.31, f32[256]{0:T(256)S(1)} %broadcast_multiply_fusion.8, f32[1280]{0:T(1024)S(1)} %copy-done.6, ...), kind=kLoop, calls=%fused_computation.96 | loop fusion | flops 2620928 | bytes 3291136 | tf_op jit(solution)/shard_map/reduce_sum | solution.py:25
  60.1 1.9 %convolution_bitcast_fusion = bf16[1,1,512,1280]{3,2,1,0:T(8,128)(2,1)} fusion(f32[256,1280]{1,0:T(8,128)S(1)} %copy-done.3, bf16[256,1280]{1,0:T(8,128)(2,1)S(1)} %multiply_convert_fusion.2.rhs_b, f32[256,1280]{1,0:T(8,128)S(1)} %get-tuple-element.31, f32[256]{0:T(256)S(1)} %broadcast_multiply_fusion.3, f32[256]{0:T(256)S(1)} %broadcast_multiply_fusion.4, ...), kind=kOutput, calls=%fused_computation.8 | convolution fusion | flops 338624512 | bytes 4593664 | tf_op jit(solution)/shard_map/dot_general | solution.py:411
  62.1 1.3 copy.37
  63.4 0.9 copy.38
  64.3 93.4 %shard_map.201 = (bf16[4,5,32,640]{3,2,1,0:T(8,128)(2,1)}, bf16[4,5,16,1280]{3,2,1,0:T(8,128)(2,1)}) custom-call(bf16[5,2,128,256]{3,2,1,0:T(8,128)(2,1)} %bitcast.68, bf16[4,256,640]{2,1,0:T(8,128)(2,1)} %bitcast.66, bf16[5,2,4,64,256]{4,3,2,1,0:T(8,128)(2,1)} %bitcast.65, bf16[256,1280]{1,0:T(8,128)(2,1)} %copy-done.2), custom_call_target="tpu_custom_call" | custom-call | tf_op jit(solution)/shard_map/pallas_call | solution.py:324
  157.7 1.3 convert_multiply_fusion.1
  159.0 1.3 copy.45
  160.4 1.3 convert_multiply_fusion
  (44 shorter events, 0.2 us)
Async XLA Ops:
  0.6 24.5 %copy-start = (bf16[1280,512]{1,0:T(8,128)(2,1)S(1)}, bf16[1280,512]{1,0:T(8,128)(2,1)}, u32[]{:S(2)}) copy-start(bf16[1280,512]{1,0:T(8,128)(2,1)} %param.30) | copy-start | bytes 3932164
  5.4 0.7 copy-start.6
  5.4 0.7 copy-start.7
  5.5 0.7 copy-start.11
  15.4 2.6 %copy-start.12 = (f32[1280]{0:T(1024)S(1)}, f32[1280]{0:T(1024)}, u32[]{:S(2)}) copy-start(f32[1280]{0:T(1024)} %param.27) | copy-start | bytes 15364
  23.7 1.1 copy-start.4
  23.7 1.4 copy-start.13
  23.8 1.3 copy-start.14
  23.8 1.3 copy-start.15
  23.8 1.3 copy-start.16
  25.1 3.2 %copy-start.8 = (s32[1,1,512]{2,1,0:T(1,128)S(1)}, s32[1,1,512]{2,1,0:T(1,128)}, u32[]{:S(2)}) copy-start(s32[1,1,512]{2,1,0:T(1,128)} %param.20) | copy-start | bytes 6148
  28.3 2.3 %copy-start.9 = (f32[512]{0:T(512)S(1)}, f32[512]{0:T(512)}, u32[]{:S(2)}) copy-start(f32[512]{0:T(512)} %param.35) | copy-start | bytes 6148
  28.3 2.3 %copy-start.10 = (f32[512]{0:T(512)S(1)}, f32[512]{0:T(512)}, u32[]{:S(2)}) copy-start(f32[512]{0:T(512)} %param.34) | copy-start | bytes 6148
  30.4 1.4 copy-start.1
  35.6 2.5 %copy-start.17 = (f32[256,2560]{1,0:T(8,128)S(1)}, f32[256,2560]{1,0:T(8,128)}, u32[]{:S(2)}) copy-start(f32[256,2560]{1,0:T(8,128)} %get-tuple-element.38) | copy-start | bytes 7864324
  38.1 22.1 %copy-start.2 = (bf16[256,1280]{1,0:T(8,128)(2,1)}, bf16[256,1280]{1,0:T(8,128)(2,1)S(1)}, u32[]{:S(2)}) copy-start(bf16[256,1280]{1,0:T(8,128)(2,1)S(1)} %multiply_convert_fusion.2.rhs_b) | copy-start | bytes 1966084
  57.5 2.6 %copy-start.3 = (f32[256,1280]{1,0:T(8,128)S(1)}, f32[256,1280]{1,0:T(8,128)}, u32[]{:S(2)}) copy-start(f32[256,1280]{1,0:T(8,128)} %convolution_multiply_fusion.1) | copy-start | bytes 3932164
  159.0 1.4 copy-start.5

commit v3 on v2

--- a/solution.py
+++ b/solution.py
@@ -116,6 +116,10 @@
     rhs_b,
     out_a,
     out_b,
+    turned_a,
+    turned_b,
+    gathered_a,
+    gathered_b,
     acc_a,
     acc_b,
     send0_a,
@@ -158,9 +162,9 @@
     pl.semaphore_wait(barrier, len(peers))
 
     tensors = (
-        (lhs_a, rhs_a, out_a, acc_a, send0_a, land0_a, send1_a, land1_a, send2_a, land2_a,
+        (turned_a, rhs_a, gathered_a, acc_a, send0_a, land0_a, send1_a, land1_a, send2_a, land2_a,
          send3_a, land3_a, x, y, across_x, across_y),
-        (lhs_b, rhs_b, out_b, acc_b, send0_b, land0_b, send1_b, land1_b, send2_b, land2_b,
+        (turned_b, rhs_b, gathered_b, acc_b, send0_b, land0_b, send1_b, land1_b, send2_b, land2_b,
          send3_b, land3_b, y, x, across_y, across_x),
     )
     copies = {}
@@ -179,22 +183,23 @@
 
     def products(t, j, which, store):
         lhs, rhs = tensors[t][0], tensors[t][1]
-        if t == 0:
-            m = lhs.shape[2] // z_count
-
-            @pl.loop(0, 4)
-            def _(e):
-                part = jnp.dot(lhs[j, which], rhs[e], preferred_element_type=jnp.float32)
-                for z in range(z_count):
-                    store(lax.div(e, 2), lax.rem(e, 2), z, part[z * m : (z + 1) * m])
-        else:
-            m = lhs.shape[3] // z_count
-
-            @pl.loop(0, 4)
-            def _(e):
-                part = jnp.dot(lhs[j, which, e], rhs[...], preferred_element_type=jnp.float32)
-                for z in range(z_count):
-                    store(lax.div(e, 2), lax.rem(e, 2), z, part[z * m : (z + 1) * m])
+        rows = lhs.shape[0] // (2 * z_count)
+        columns = rhs.shape[1] // chunks
+
+        @pl.loop(0, z_count)
+        def _(z):
+            first = pl.multiple_of((2 * z + which) * rows, 16)
+            part = jnp.dot(
+                lhs[pl.ds(first, rows), :],
+                rhs[:, j * columns : (j + 1) * columns],
+                preferred_element_type=jnp.float32,
+            )
+            for e in range(4):
+                if t == 0:
+                    width = columns // 4
+                    store(e // 2, e % 2, z, part[:, e * width : (e + 1) * width])
+                else:
+                    store(e // 2, e % 2, z, part[e * (rows // 4) : (e + 1) * (rows // 4)])
 
     def stage0(t, j):
         acc, send0, land0 = tensors[t][3:6]
@@ -205,6 +210,10 @@
         def store_own(f, g, z, value):
             acc[j, f, g, z] = value
 
+        if j == 0:
+            source = (lhs_a, lhs_b)[t]
+            for at in range(0, source.shape[1], 256):
+                tensors[t][0][at : at + 256, :] = source[:, at : at + 256].T
         products(t, j, 1 - core, store_send)
         send(("c", t, j), send0.at[j], land0.at[j], pair_sems, (0, t, j), sibling)
         products(t, j, core, store_own)
@@ -274,17 +283,24 @@
                 ("s", t, j, k), out.at[mine, j], out.at[mine, j], spread_sems, (t, j, k), peer
             )
 
-    stages = (stage0, stage1, stage2, stage3, stage4)
+    def stage5(t, j):
+        gathered = tensors[t][2]
+        for k in range(3):
+            copies["s", t, j, k].wait()
+        m, n = gathered.shape[2:]
+        for e in range(4):
+            if t == 0:
+                out_a[:, (4 * j + e) * n : (4 * j + e + 1) * n] = gathered[e, j]
+            else:
+                out_b[e * m : (e + 1) * m, j * n : (j + 1) * n] = gathered[e, j]
+
+    stages = (stage0, stage1, stage2, stage3, stage4, stage5)
     for step in range(chunks + len(stages) - 1):
         for at in reversed(range(len(stages))):
             j = step - at
             if 0 <= j < chunks:
                 for t in range(2):
                     stages[at](t, j)
-    for j in range(chunks):
-        for t in range(2):
-            for k in range(3):
-                copies["s", t, j, k].wait()
 
 
 def reduce_weights(mlp_in, grad_pre, hidden, grad_encoded, tiles):
@@ -293,16 +309,16 @@
     z_count = tiles // 2
     rows_a, rows_b = width // tiles, inner // tiles // 4
     chunks = 5
-    m_a, n_a = rows_a // chunks, inner // 4
-    m_b, n_b = rows_b // chunks, width
-    lhs_a = mlp_in.T.reshape(z_count, 2, chunks, m_a, rows).transpose(2, 1, 0, 3, 4)
-    lhs_a = lhs_a.reshape(chunks, 2, z_count * m_a, rows)
-    rhs_a = grad_pre.reshape(rows, 4, n_a).transpose(1, 0, 2)
-    lhs_b = hidden.T.reshape(z_count, 2, 4, chunks, m_b, rows).transpose(3, 1, 2, 0, 4, 5)
-    lhs_b = lhs_b.reshape(chunks, 2, 4, z_count * m_b, rows)
+    m_a, n_a = rows_a, inner // chunks // 4
+    m_b, n_b = rows_b, width // chunks
     whole = pl.BlockSpec(memory_space=pltpu.VMEM)
     half, full = jnp.bfloat16, jnp.float32
-    scratch = []
+    scratch = [
+        pltpu.VMEM((width, rows), half),
+        pltpu.VMEM((inner, rows), half),
+        pltpu.VMEM((4, chunks, m_a, n_a), half),
+        pltpu.VMEM((4, chunks, m_b, n_b), half),
+    ]
     for lead, kind in (
         ((2, 2, z_count), full),
         ((2, 2, z_count), half),
@@ -324,8 +340,8 @@
     out_a, out_b = pl.pallas_call(
         functools.partial(reduce_kernel, chunks, z_count),
         out_shape=(
-            jax.ShapeDtypeStruct((4, chunks, m_a, n_a), half),
-            jax.ShapeDtypeStruct((4, chunks, m_b, n_b), half),
+            jax.ShapeDtypeStruct((rows_a, inner), half),
+            jax.ShapeDtypeStruct((4 * rows_b, width), half),
         ),
         in_specs=[whole] * 4,
         out_specs=(whole, whole),
@@ -333,10 +349,8 @@
         compiler_params=pltpu.CompilerParams(
             collective_id=0, has_side_effects=True, vmem_limit_bytes=56 * 2**20
         ),
-    )(lhs_a, rhs_a, lhs_b, grad_encoded)
-    fc1 = out_a.reshape(4, rows_a, n_a).transpose(1, 0, 2).reshape(rows_a, inner)
-    fc2 = out_b.reshape(4 * rows_b, n_b)
-    return fc1.astype(full), fc2.astype(full)
+    )(mlp_in, grad_pre, hidden, grad_encoded)
+    return out_a.astype(full), out_b.astype(full)
 
 
 def reducible(mlp_in, hidden, scenes, tiles):
@@ -344,10 +358,10 @@
     return (
         scenes == 4
         and tiles % 2 == 0
-        and width % (tiles * 5 * 16) == 0
-        and inner % (tiles * 4 * 5 * 16) == 0
-        and inner % (4 * 128) == 0
-        and width % 128 == 0
+        and width % (tiles * 16) == 0
+        and inner % (tiles * 4 * 16) == 0
+        and inner % (5 * 4 * 128) == 0
+        and width % (5 * 128) == 0
     )
 
 

time: 162 us -> 143 us (0.88)
  local copies, waits for them, and re-layouts: 18.5 us -> 5.19 us
  matrix products: 37.9 us -> 32.9 us
  other arithmetic: 11.1 us -> 9.15 us
    convert_element_type x3 -> x0, local copies, waits for them, and re-layouts: 6.15 us -> none  [the longest x1 2.42 us: encode(): hidden = activation.astype(jnp.bfloat16)]
    dot_general x1, matrix products: 5.74 us -> 1.96 us  [encode(): jnp.dot(hidden, fc2_weight, preferred_element_type=jnp.float32)]
    transpose x2 -> x0, local copies, waits for them, and re-layouts: 3.47 us -> none  [the longest x1 2.57 us: reduce_weights(): hidden.T.reshape(z_count, 2, 4, chunks, m_b, rows)]
    reduce_sum x2 -> x1, other arithmetic: 3.8 us -> 0.38 us  [norm_back(): mean_up = jnp.mean(upstream, axis=-1, keepdims=True)]
    reshape x1 -> x0, local copies, waits for them, and re-layouts: 2.43 us -> none  [reduce_weights(): rhs_a = grad_pre.reshape(rows, 4, n_a).transpose(1, 0, 2)]
    unnamed x38 -> x52, local copies, waits for them, and re-layouts: 5.06 us -> 5.19 us
where the time goes in v3:
time: 143 us; the launch traced here: 142 us
  Pallas kernels  93.9 us (66%)
  matrix products  32.9 us (23%)
  other arithmetic  9.15 us (6%)
  local copies, waits for them, and re-layouts  5.19 us (4%)
    pallas_call x1, Pallas kernels, reduce_weights(): pl.pallas_call(functools.partial(reduce_kernel, chunks, z_count), out_sha...  93.9 us
    dot_general x1, matrix products, encode(): jnp.dot(mlp_in, fc1_weight, preferred_element_type=jnp.float32) + fc1_bias  6.73 us
    dot_general x1, matrix products, encode_back(): jnp.dot(grad_encoded, fc2_weight.T, preferred_element_type=jnp.float32)  6.28 us
    unnamed x52, local copies, waits for them, and re-layouts  5.19 us
    dot_general x1, matrix products, encode_back(): jnp.dot(grad_pre, fc1_weight.T, preferred_element_type=jnp.float32)  4.95 us
    dot_general x1, matrix products, encode_back(): jnp.dot(grad_compact, embed_weight.T, preferred_element_type=jnp.float32)  3.92 us
    div x2, other arithmetic, shards(): fc1_grad, fc2_grad = [total / device_total for total in totals]  3.83 us
    dot_general x1, matrix products, shards(): jnp.dot(scatter, projected, preferred_element_type=jnp.float32)  3.23 us

profile of v3, /device:TPU:0, one launch (start us, length us, event | category | flops | bytes accessed | tf_op | source)
XLA Modules:
  0.0 142.1 jit_solution(5185752200686940723)
XLA Ops:
  0.6 0.0 copy-start
  0.6 0.9 select_reduce_fusion
  1.6 0.7 broadcast_select_fusion
  2.3 2.0 %copy.24 = bf16[1,1,512,512]{2,3,1,0:T(8,128)(2,1)} copy(bf16[1,1,512,512]{3,2,1,0:T(8,128)(2,1)} %param.21) | data formatting | bytes 1048576 | tf_op args[3]
  4.3 1.9 %fusion.60 = (f32[256]{0:T(256)S(1)}, f32[256,1280]{1,0:T(8,128)S(1)}) fusion(bf16[1,1,512,1280]{3,2,1,0:T(8,128)(2,1)} %param.18, s32[512]{0:T(512)S(1)} %get-tuple-element.22), kind=kOutput, calls=%fused_computation.91 | convolution fusion | flops 336330496 | bytes 2624512 | tf_op jit(solution)/shard_map/dot_general | solution.py:415
  6.3 0.3 multiply_reduce_fusion.3
  6.6 0.4 copy-done.11
  6.9 0.0 copy-done.12
  6.9 0.3 add_convert_fusion.2.lhs_a
  7.3 0.0 slice-start.1
  7.3 0.0 copy-start.17
  7.3 6.7 %multiply_convert_fusion = (bf16[256,2560]{1,0:T(8,128)(2,1)S(1)}, f32[256,2560]{1,0:T(8,128)}) fusion(f32[2560]{0:T(1024)S(1)} %copy-done.16, bf16[256,1280]{1,0:T(8,128)(2,1)S(1)} %add_convert_fusion.2.lhs_a, bf16[1280,2560]{1,0:T(8,128)(2,1)} %param.24), kind=kOutput, calls=%fused_computation.13 | convolution fusion | flops 1681653760 | bytes 11151360 | tf_op jit(solution)/shard_map/dot_general | solution.py:52
  14.1 2.0 %fusion.61 = (f32[256]{0:T(256)S(1)}, f32[256,1280]{1,0:T(8,128)S(1)}) fusion(f32[1280]{0:T(1024)S(1)} %copy-done.17, f32[256,1280]{1,0:T(8,128)S(1)} %get-tuple-element.26, bf16[256,2560]{1,0:T(8,128)(2,1)S(1)} %get-tuple-element.27.lhs_b, bf16[2560,1280]{1,0:T(8,128)(2,1)S(1)} %bitcast.37), kind=kOutput, calls=%fused_computation.92 | convolution fusion | flops 1678704384 | bytes 10491904 | tf_op jit(solution)/shard_map/dot_general | solution.py:55
  16.0 0.0 copy-start.4
  16.0 0.0 copy-start.18
  16.1 1.0 copy-done.4
  17.1 0.3 multiply_reduce_fusion.2
  17.4 3.2 %convolution_select_fusion = f32[512,512]{0,1:T(8,128)} fusion(bf16[1280,512]{1,0:T(8,128)(2,1)S(1)} %copy-done, f32[256,1280]{1,0:T(8,128)} %copy-done.4, f32[1280]{0:T(1024)S(1)} %copy-done.18, f32[1280]{0:T(1024)S(1)} %copy-done.19, f32[256]{0:T(256)S(1)} %add_rsqrt_fusion.1, f32[256]{0:T(256)S(1)} %broadcast_multiply_fusion.7, f32[512]{0:T(512)S(1)} %copy-done.20, ...), kind=kOutput, calls=%fused_computation.19 | convolution fusion | flops 472055808 | bytes 3688960 | tf_op jit(solution)/shard_map/dot_general | solution.py:417
  20.7 1.9 %fusion.62 = (f32[512]{0:T(512)S(1)}, f32[512,512]{0,1:T(8,128)S(1)}) fusion(f32[512,512]{0,1:T(8,128)} %convolution_select_fusion, bf16[512,512]{1,0:T(8,128)(2,1)S(1)} %copy-done.10, s32[512]{0:T(512)S(1)} %bitcast.35), kind=kOutput, calls=%fused_computation.93 | convolution fusion | flops 269221376 | bytes 2625536 | tf_op jit(solution)/shard_map/dot_general | solution.py:102
  22.6 0.2 multiply_reduce_fusion.4
  22.9 0.4 fusion.12
  23.2 0.4 copy-done.1
  23.6 3.9 %fusion.59 = (f32[256]{0:T(256)S(1)}, f32[256]{0:T(256)S(1)}, f32[256,1280]{1,0:T(8,128)}) fusion(f32[256]{0:T(256)S(1)} %add_rsqrt_fusion.1, f32[256,1280]{1,0:T(8,128)} %copy-done.4, f32[256]{0:T(256)S(1)} %broadcast_multiply_fusion.7, f32[1280]{0:T(1024)S(1)} %copy-done.19, bf16[1280,512]{1,0:T(8,128)(2,1)S(1)} %copy-done, f32[512,512]{0,1:T(8,128)} %copy-done.1, ...), kind=kOutput, calls=%fused_computation.90 | convolution fusion | flops 474480128 | bytes 5527040 | tf_op jit(solution)/shard_map/dot_general | solution.py:79
  27.6 2.2 %multiply_convert_fusion.1.rhs_b = bf16[256,1280]{1,0:T(8,128)(2,1)S(1)} fusion(f32[256,1280]{1,0:T(8,128)} %get-tuple-element.33, f32[256,1280]{1,0:T(8,128)} %copy-done.4, f32[256]{0:T(256)S(1)} %broadcast_multiply_fusion.5, f32[256]{0:T(256)S(1)} %broadcast_multiply_fusion.6, f32[256]{0:T(256)S(1)} %add_rsqrt_fusion.1, f32[256]{0:T(256)S(1)} %broadcast_multiply_fusion.7), kind=kLoop, calls=%fused_computation.23 | loop fusion | flops 2293760 | bytes 3280896 | tf_op jit(solution)/shard_map/convert_element_type | solution.py:80
  29.8 0.3 copy-done.22
  30.1 6.3 %fusion.rhs_a = bf16[256,2560]{1,0:T(8,128)(2,1)} fusion(bf16[256,1280]{1,0:T(8,128)(2,1)S(1)} %multiply_convert_fusion.1.rhs_b, bf16[2560,1280]{1,0:T(8,128)(2,1)} %param.26, f32[256,2560]{1,0:T(8,128)S(1)} %copy-done.22), kind=kOutput, calls=%fused_computation.3 | convolution fusion | flops 1684275200 | bytes 11141120 | tf_op jit(solution)/shard_map/dot_general | solution.py:81
  36.4 93.9 %shard_map.201 = (bf16[160,2560]{1,0:T(8,128)(2,1)}, bf16[320,1280]{1,0:T(8,128)(2,1)}) custom-call(bf16[256,1280]{1,0:T(8,128)(2,1)} %copy-done.5, bf16[256,2560]{1,0:T(8,128)(2,1)} %fusion.rhs_a, bf16[256,2560]{1,0:T(8,128)(2,1)} %copy-done.7, bf16[256,1280]{1,0:T(8,128)(2,1)} %copy-done.2), custom_call_target="tpu_custom_call" | custom-call | tf_op jit(solution)/shard_map/pallas_call | solution.py:340
  130.3 5.0 %fusion.58 = (f32[256]{0:T(256)S(1)}, f32[256]{0:T(256)S(1)}, f32[256,1280]{1,0:T(8,128)S(1)}) fusion(f32[256]{0:T(256)S(1)} %add_rsqrt_fusion.2, f32[256,1280]{1,0:T(8,128)S(1)} %get-tuple-element.26, f32[256]{0:T(256)S(1)} %broadcast_multiply_fusion.8, f32[1280]{0:T(1024)S(1)} %copy-done.12, bf16[256,2560]{1,0:T(8,128)(2,1)S(1)} %copy-done.8, ...), kind=kOutput, calls=%fused_computation.89 | convolution fusion | flops 1679687168 | bytes 10494976 | tf_op jit(solution)/shard_map/dot_general | solution.py:83
  135.3 2.0 %convolution_bitcast_fusion = bf16[1,1,512,1280]{3,2,1,0:T(8,128)(2,1)} fusion(f32[256,1280]{1,0:T(8,128)S(1)} %get-tuple-element.34, bf16[256,1280]{1,0:T(8,128)(2,1)S(1)} %copy-done.3, f32[256,1280]{1,0:T(8,128)S(1)} %get-tuple-element.26, f32[256]{0:T(256)S(1)} %broadcast_multiply_fusion.3, f32[256]{0:T(256)S(1)} %broadcast_multiply_fusion.4, ...), kind=kOutput, calls=%fused_computation.8 | convolution fusion | flops 338624512 | bytes 4593664 | tf_op jit(solution)/shard_map/dot_general | solution.py:425
  137.3 1.0 copy.25
  138.3 2.6 %convert_multiply_fusion.1 = f32[160,2560]{1,0:T(8,128)} fusion(bf16[160,2560]{1,0:T(8,128)(2,1)} %get-tuple-element.6), kind=kLoop, calls=%fused_computation.17 | loop fusion | flops 819200 | bytes 2457600 | tf_op jit(solution)/shard_map/div | solution.py:438
  140.9 1.3 convert_multiply_fusion
  (52 shorter events, 0.1 us)
Async XLA Ops:
  0.6 16.7 %copy-start = (bf16[1280,512]{1,0:T(8,128)(2,1)S(1)}, bf16[1280,512]{1,0:T(8,128)(2,1)}, u32[]{:S(2)}) copy-start(bf16[1280,512]{1,0:T(8,128)(2,1)} %param.30) | copy-start | bytes 3932164
  6.2 0.7 copy-start.11
  6.2 0.7 copy-start.12
  6.5 0.7 copy-start.16
  6.9 7.1 %slice-start = ((s8[6553600]{0:T(1024)(128)(4,1)}), s8[4194304]{0:T(1024)(128)(4,1)S(1)}, s32[]{:S(2)}) async-start(s8[6553600]{0:T(1024)(128)(4,1)} %bitcast.36), calls=%async_computation | async-start | bytes 8388608
  7.3 6.8 %copy-start.5 = (bf16[256,1280]{1,0:T(8,128)(2,1)}, bf16[256,1280]{1,0:T(8,128)(2,1)S(1)}, u32[]{:S(2)}) copy-start(bf16[256,1280]{1,0:T(8,128)(2,1)S(1)} %add_convert_fusion.2.lhs_a) | copy-start | bytes 1966084
  7.3 6.8 %slice-start.1 = ((s8[6553600]{0:T(1024)(128)(4,1)}), s8[2359296]{0:T(1024)(128)(4,1)S(1)}, s32[]{:S(2)}) async-start(s8[6553600]{0:T(1024)(128)(4,1)} %bitcast.36), calls=%async_computation.1 | async-start | bytes 4718592
  7.3 6.8 %copy-start.17 = (f32[1280]{0:T(1024)S(1)}, f32[1280]{0:T(1024)}, u32[]{:S(2)}) copy-start(f32[1280]{0:T(1024)} %param.27) | copy-start | bytes 15364
  14.0 2.0 %copy-start.7 = (bf16[256,2560]{1,0:T(8,128)(2,1)}, bf16[256,2560]{1,0:T(8,128)(2,1)S(1)}, u32[]{:S(2)}) copy-start(bf16[256,2560]{1,0:T(8,128)(2,1)S(1)} %get-tuple-element.27.lhs_b) | copy-start | bytes 3932164
  16.0 1.1 copy-start.4
  16.0 1.3 copy-start.18
  16.0 1.3 copy-start.19
  16.1 1.3 copy-start.20
  16.1 1.3 copy-start.21
  17.4 3.3 %copy-start.10 = (bf16[512,512]{1,0:T(8,128)(2,1)S(1)}, bf16[512,512]{1,0:T(8,128)(2,1)}, u32[]{:S(2)}) copy-start(bf16[512,512]{1,0:T(8,128)(2,1)} %param.33) | copy-start | bytes 1572868
  17.4 3.2 %copy-start.13 = (s32[1,1,512]{2,1,0:T(1,128)S(1)}, s32[1,1,512]{2,1,0:T(1,128)}, u32[]{:S(2)}) copy-start(s32[1,1,512]{2,1,0:T(1,128)} %param.20) | copy-start | bytes 6148
  20.7 2.2 %copy-start.6 = (bf16[1,1,512,512]{2,3,1,0:T(8,128)(2,1)S(1)}, bf16[1,1,512,512]{2,3,1,0:T(8,128)(2,1)}, u32[]{:S(2)}) copy-start(bf16[1,1,512,512]{2,3,1,0:T(8,128)(2,1)} %copy.24) | copy-start | bytes 1572868
  20.7 2.2 %copy-start.14 = (f32[512]{0:T(512)S(1)}, f32[512]{0:T(512)}, u32[]{:S(2)}) copy-start(f32[512]{0:T(512)} %param.35) | copy-start | bytes 6148
  20.7 2.2 %copy-start.15 = (f32[512]{0:T(512)S(1)}, f32[512]{0:T(512)}, u32[]{:S(2)}) copy-start(f32[512]{0:T(512)} %param.34) | copy-start | bytes 6148
  22.6 1.0 copy-start.1
  27.6 2.5 %copy-start.22 = (f32[256,2560]{1,0:T(8,128)S(1)}, f32[256,2560]{1,0:T(8,128)}, u32[]{:S(2)}) copy-start(f32[256,2560]{1,0:T(8,128)} %get-tuple-element.28) | copy-start | bytes 7864324
  30.1 6.3 %copy-start.2 = (bf16[256,1280]{1,0:T(8,128)(2,1)}, bf16[256,1280]{1,0:T(8,128)(2,1)S(1)}, u32[]{:S(2)}) copy-start(bf16[256,1280]{1,0:T(8,128)(2,1)S(1)} %multiply_convert_fusion.1.rhs_b) | copy-start | bytes 1966084
  36.4 94.0 %copy-start.8 = (bf16[256,2560]{1,0:T(8,128)(2,1)S(1)}, bf16[256,2560]{1,0:T(8,128)(2,1)}, u32[]{:S(2)}) copy-start(bf16[256,2560]{1,0:T(8,128)(2,1)} %fusion.rhs_a) | copy-start | bytes 3932164
  130.3 5.0 %copy-start.3 = (bf16[256,1280]{1,0:T(8,128)(2,1)S(1)}, bf16[256,1280]{1,0:T(8,128)(2,1)}, u32[]{:S(2)}) copy-start(bf16[256,1280]{1,0:T(8,128)(2,1)} %copy-done.2) | copy-start | bytes 1966084
  138.3 2.6 %copy-start.9 = (bf16[320,1280]{1,0:T(8,128)(2,1)S(1)}, bf16[320,1280]{1,0:T(8,128)(2,1)}, u32[]{:S(2)}) copy-start(bf16[320,1280]{1,0:T(8,128)(2,1)} %get-tuple-element.7) | copy-start | bytes 2457604

commit v4 on v3

--- a/solution.py
+++ b/solution.py
@@ -114,8 +114,17 @@
     rhs_a,
     lhs_b,
     rhs_b,
+    weight,
+    gain,
+    scaled,
+    inverse,
+    scatter,
     out_a,
     out_b,
+    feature_out,
+    weight_held,
+    upstream,
+    grad_rows,
     turned_a,
     turned_b,
     gathered_a,
@@ -126,21 +135,16 @@
     send0_b,
     land0_a,
     land0_b,
-    send1_a,
-    send1_b,
     land1_a,
     land1_b,
-    send2_a,
-    send2_b,
     land2_a,
     land2_b,
-    send3_a,
-    send3_b,
     land3_a,
     land3_b,
     pair_sems,
     z_sems,
     spread_sems,
+    weight_sem,
 ):
     dp = lax.axis_index("dp")
     tile = lax.axis_index("tile")
@@ -156,16 +160,18 @@
     peers = [sibling, across_x, across_y, diagonal]
     peers += [(dp, 2 * z + core) for z in z_to]
 
+    fetch = pltpu.make_async_copy(weight, weight_held, weight_sem)
+    fetch.start()
     barrier = pltpu.get_barrier_semaphore()
     for peer in peers:
         pl.semaphore_signal(barrier, inc=1, device_id=peer, device_id_type=MESH)
     pl.semaphore_wait(barrier, len(peers))
 
     tensors = (
-        (turned_a, rhs_a, gathered_a, acc_a, send0_a, land0_a, send1_a, land1_a, send2_a, land2_a,
-         send3_a, land3_a, x, y, across_x, across_y),
-        (turned_b, rhs_b, gathered_b, acc_b, send0_b, land0_b, send1_b, land1_b, send2_b, land2_b,
-         send3_b, land3_b, y, x, across_y, across_x),
+        (turned_a, rhs_a, gathered_a, acc_a, send0_a, land0_a, send0_a, land1_a, send0_a, land2_a,
+         send0_a, land3_a, x, y, across_x, across_y),
+        (turned_b, rhs_b, gathered_b, acc_b, send0_b, land0_b, send0_b, land1_b, send0_b, land2_b,
+         send0_b, land3_b, y, x, across_y, across_x),
     )
     copies = {}
 
@@ -226,11 +232,11 @@
         @pl.loop(0, z_count)
         def _(z):
             for g in range(2):
-                send1[j, g, z] = (
+                send1[j, 0, g, z] = (
                     acc[j, 1 - f, g, z] + land0[j, 1 - f, g, z].astype(jnp.float32)
                 ).astype(jnp.bfloat16)
 
-        send(("f", t, j), send1.at[j], land1.at[j], pair_sems, (1, t, j), partner)
+        send(("f", t, j), send1.at[j, 0], land1.at[j], pair_sems, (1, t, j), partner)
 
         @pl.loop(0, z_count)
         def _(z):
@@ -245,11 +251,11 @@
 
         @pl.loop(0, z_count)
         def _(z):
-            send2[j, z] = (
+            send2[j, 1, 0, z] = (
                 acc[j, f, 1 - g, z] + land1[j, 1 - g, z].astype(jnp.float32)
             ).astype(jnp.bfloat16)
 
-        send(("g", t, j), send2.at[j], land2.at[j], pair_sems, (2, t, j), partner)
+        send(("g", t, j), send2.at[j, 1, 0], land2.at[j], pair_sems, (2, t, j), partner)
 
         @pl.loop(0, z_count)
         def _(z):
@@ -261,9 +267,9 @@
         f, g = tensors[t][12], tensors[t][13]
         copies["g", t, j].wait()
         for k, z in enumerate(z_to):
-            send3[j, k] = (acc[j, f, g, z] + land2[j, z].astype(jnp.float32)).astype(jnp.bfloat16)
+            send3[j, 1, 1, k] = (acc[j, f, g, z] + land2[j, z].astype(jnp.float32)).astype(jnp.bfloat16)
             send(
-                ("z", t, j, k), send3.at[j, k], land3.at[j, k], z_sems, (t, j, k),
+                ("z", t, j, k), send3.at[j, 1, 1, k], land3.at[j, k], z_sems, (t, j, k),
                 (dp, 2 * z + core),
             )
         acc[j, f, g, my_z] = acc[j, f, g, my_z] + land2[j, my_z].astype(jnp.float32)
@@ -294,6 +300,37 @@
             else:
                 out_b[e * m : (e + 1) * m, j * n : (j + 1) * n] = gathered[e, j]
 
+    def feature_columns(q):
+        if q == 0:
+            fetch.wait()
+        wide = weight_held.shape[0] // chunks
+        at = slice(q * wide, (q + 1) * wide)
+        part = lax.dot_general(
+            rhs_a[...],
+            weight_held[at, :],
+            (((1,), (1,)), ((), ())),
+            preferred_element_type=jnp.float32,
+        )
+        upstream[:, at] = part * gain[:, at]
+
+    def feature_rows():
+        block = upstream.shape[0] // 8
+
+        @pl.loop(0, 8)
+        def _(i):
+            at = pl.ds(pl.multiple_of(i * block, block), block)
+            back = norm_back(upstream[at, :], scaled[at, :], inverse[at, :])
+            grad_rows[at, :] = (rhs_b[at, :].astype(jnp.float32) + back).astype(jnp.bfloat16)
+
+        tall = feature_out.shape[0] // 4
+
+        @pl.loop(0, 4)
+        def _(i):
+            at = pl.ds(pl.multiple_of(i * tall, tall), tall)
+            feature_out[at, :] = jnp.dot(
+                scatter[at, :], grad_rows[...], preferred_element_type=jnp.float32
+            ).astype(jnp.bfloat16)
+
     stages = (stage0, stage1, stage2, stage3, stage4, stage5)
     for step in range(chunks + len(stages) - 1):
         for at in reversed(range(len(stages))):
@@ -301,9 +338,15 @@
             if 0 <= j < chunks:
                 for t in range(2):
                     stages[at](t, j)
-
-
-def reduce_weights(mlp_in, grad_pre, hidden, grad_encoded, tiles):
+        if 1 <= step <= chunks:
+            feature_columns(step - 1)
+        if step == chunks + 1:
+            feature_rows()
+
+
+def reduce_weights(
+    mlp_in, grad_pre, hidden, grad_encoded, tiles, fc1_weight, mlp_gain, mlp_scaled, mlp_inv, scatter
+):
     rows, width = mlp_in.shape
     inner = hidden.shape[1]
     z_count = tiles // 2
@@ -314,6 +357,9 @@
     whole = pl.BlockSpec(memory_space=pltpu.VMEM)
     half, full = jnp.bfloat16, jnp.float32
     scratch = [
+        pltpu.VMEM((width, inner), half),
+        pltpu.VMEM((rows, width), full),
+        pltpu.VMEM((rows, width), half),
         pltpu.VMEM((width, rows), half),
         pltpu.VMEM((inner, rows), half),
         pltpu.VMEM((4, chunks, m_a, n_a), half),
@@ -324,10 +370,7 @@
         ((2, 2, z_count), half),
         ((2, 2, z_count), half),
         ((2, z_count), half),
-        ((2, z_count), half),
         ((z_count,), half),
-        ((z_count,), half),
-        ((z_count - 1,), half),
         ((z_count - 1,), half),
     ):
         for m, n in ((m_a, n_a), (m_b, n_b)):
@@ -336,21 +379,33 @@
         pltpu.SemaphoreType.DMA((2, 3, 2, chunks)),
         pltpu.SemaphoreType.DMA((2, 2, chunks, z_count - 1)),
         pltpu.SemaphoreType.DMA((2, 2, chunks, 3)),
+        pltpu.SemaphoreType.DMA,
     ]
-    out_a, out_b = pl.pallas_call(
+    out_a, out_b, features = pl.pallas_call(
         functools.partial(reduce_kernel, chunks, z_count),
         out_shape=(
             jax.ShapeDtypeStruct((rows_a, inner), half),
             jax.ShapeDtypeStruct((4 * rows_b, width), half),
+            jax.ShapeDtypeStruct((scatter.shape[0], width), half),
         ),
-        in_specs=[whole] * 4,
-        out_specs=(whole, whole),
+        in_specs=[whole] * 4 + [pl.BlockSpec(memory_space=pl.ANY)] + [whole] * 4,
+        out_specs=(whole, whole, whole),
         scratch_shapes=scratch,
         compiler_params=pltpu.CompilerParams(
             collective_id=0, has_side_effects=True, vmem_limit_bytes=56 * 2**20
         ),
-    )(mlp_in, grad_pre, hidden, grad_encoded)
-    return out_a.astype(full), out_b.astype(full)
+    )(
+        mlp_in,
+        grad_pre,
+        hidden,
+        grad_encoded,
+        fc1_weight,
+        mlp_gain[None, :],
+        mlp_scaled,
+        mlp_inv,
+        scatter,
+    )
+    return (out_a.astype(full), out_b.astype(full)), features
 
 
 def reducible(mlp_in, hidden, scenes, tiles):
@@ -422,12 +477,23 @@
     mlp_in, grad_pre, hidden, grad_encoded, grad_feats = encode_back(
         saved, grad_compact, enc_params
     )
-    grad_rows = jnp.dot(scatter, grad_feats, preferred_element_type=jnp.bfloat16)
     device_total = lax.axis_size("dp") * lax.axis_size("tile")
     tiles = lax.axis_size("tile")
     if reducible(mlp_in, hidden, lax.axis_size("dp"), tiles):
-        totals = reduce_weights(mlp_in, grad_pre, hidden, grad_encoded, tiles)
+        totals, grad_rows = reduce_weights(
+            mlp_in,
+            grad_pre,
+            hidden,
+            grad_encoded,
+            tiles,
+            fc1_weight,
+            mlp_gain,
+            saved[1],
+            saved[2],
+            scatter,
+        )
     else:
+        grad_rows = jnp.dot(scatter, grad_feats, preferred_element_type=jnp.bfloat16)
         totals = []
         for left, right in ((mlp_in, grad_pre), (hidden, grad_encoded)):
             term = jnp.dot(left.T, right, preferred_element_type=jnp.float32)

time: 143 us -> 132 us (0.923)
  matrix products: 32.9 us -> 20.6 us
  other arithmetic: 9.15 us -> 11.1 us
    dot_general x2 -> x0, matrix products: 6.93 us -> none  [the longest x1 4.95 us: encode_back(): jnp.dot(grad_pre, fc1_weight.T, preferred_element_type=jnp.float32)]
    dot_general x1, matrix products: 6.73 us -> 3.28 us  [encode(): jnp.dot(mlp_in, fc1_weight, preferred_element_type=jnp.float32) + fc1_bias]
    unnamed x52 -> x51, local copies, waits for them, and re-layouts: 5.19 us -> 3.41 us
where the time goes in v4:
time: 132 us
  Pallas kernels  94.6 us (72%)
  matrix products  20.6 us (16%)
  other arithmetic  11.1 us (8%)
  local copies, waits for them, and re-layouts  4.8 us (4%)
    pallas_call x1, Pallas kernels, reduce_weights(): pl.pallas_call(functools.partial(reduce_kernel, chunks, z_count), out_sha...  94.6 us
    dot_general x1, matrix products, encode_back(): jnp.dot(grad_encoded, fc2_weight.T, preferred_element_type=jnp.float32)  6.08 us
    div x2, other arithmetic, shards(): fc1_grad, fc2_grad = [total / device_total for total in totals]  3.83 us
    dot_general x1, matrix products, encode_back(): jnp.dot(grad_compact, embed_weight.T, preferred_element_type=jnp.float32)  3.44 us
    unnamed x51, local copies, waits for them, and re-layouts  3.41 us
    dot_general x1, matrix products, encode(): jnp.dot(mlp_in, fc1_weight, preferred_element_type=jnp.float32) + fc1_bias  3.28 us

profile of v4, /device:TPU:0, one launch (start us, length us, event | category | flops | bytes accessed | tf_op | source)
XLA Modules:
  0.0 131.9 jit_solution(10057314663926281256)
XLA Ops:
  0.6 0.0 copy-start
  0.6 0.9 select_reduce_fusion
  1.6 0.7 broadcast_select_fusion
  2.3 2.1 %fusion.55 = (f32[256]{0:T(256)S(1)}, f32[256,1280]{1,0:T(8,128)S(1)}) fusion(bf16[1,1,512,1280]{3,2,1,0:T(8,128)(2,1)} %param.18, s32[512]{0:T(512)S(1)} %get-tuple-element.28), kind=kOutput, calls=%fused_computation.80 | convolution fusion | flops 336330496 | bytes 2624512 | tf_op jit(solution)/shard_map/dot_general | solution.py:470
  4.4 0.3 multiply_reduce_fusion.2
  4.7 1.4 %add_convert_fusion.1 = (bf16[256,1280]{1,0:T(8,128)(2,1)S(1)}, f32[256,1280]{1,0:T(8,128)}) fusion(f32[1280]{0:T(1024)S(1)} %copy-done.11, f32[1280]{0:T(1024)S(1)} %copy-done.10, f32[256]{0:T(256)S(1)} %add_rsqrt_fusion.2, f32[256,1280]{1,0:T(8,128)S(1)} %get-tuple-element.32, f32[256]{0:T(256)S(1)} %broadcast_multiply_fusion.6), kind=kLoop, calls=%fused_computation.23 | loop fusion | flops 1638400 | bytes 3289088 | tf_op jit(solution)/shard_map/convert_element_type | solution.py:51
  6.1 3.3 %multiply_convert_fusion = (bf16[256,2560]{1,0:T(8,128)(2,1)S(1)}, f32[256,2560]{1,0:T(8,128)}) fusion(f32[2560]{0:T(1024)S(1)} %copy-done.15, bf16[256,1280]{1,0:T(8,128)(2,1)S(1)} %get-tuple-element.26.lhs_a, bf16[1280,2560]{1,0:T(8,128)(2,1)S(1)} %copy-done.1), kind=kOutput, calls=%fused_computation.11 | convolution fusion | flops 1681653760 | bytes 11151360 | tf_op jit(solution)/shard_map/dot_general | solution.py:52
  9.4 1.9 %fusion.56 = (f32[256]{0:T(256)S(1)}, f32[256,1280]{1,0:T(8,128)S(1)}) fusion(f32[1280]{0:T(1024)S(1)} %copy-done.16, f32[256,1280]{1,0:T(8,128)S(1)} %get-tuple-element.32, bf16[256,2560]{1,0:T(8,128)(2,1)S(1)} %get-tuple-element.33.lhs_b, bf16[2560,1280]{1,0:T(8,128)(2,1)S(1)} %bitcast.37), kind=kOutput, calls=%fused_computation.81 | convolution fusion | flops 1678704384 | bytes 10491904 | tf_op jit(solution)/shard_map/dot_general | solution.py:55
  11.4 0.3 multiply_reduce_fusion.1
  11.7 0.4 copy-done.17
  12.1 0.1 copy-done.18
  12.1 0.0 copy-done.19
  12.2 0.1 copy-done.20
  12.2 1.9 %convolution_select_fusion = f32[512,512]{0,1:T(8,128)} fusion(bf16[1280,512]{1,0:T(8,128)(2,1)S(1)} %copy-done, f32[256,1280]{1,0:T(8,128)S(1)} %get-tuple-element.36, f32[1280]{0:T(1024)S(1)} %copy-done.17, f32[1280]{0:T(1024)S(1)} %copy-done.18, f32[256]{0:T(256)S(1)} %add_rsqrt_fusion.1, f32[256]{0:T(256)S(1)} %broadcast_multiply_fusion.5, ...), kind=kOutput, calls=%fused_computation.17 | convolution fusion | flops 472055808 | bytes 3688960 | tf_op jit(solution)/shard_map/dot_general | solution.py:472
  14.1 1.9 %fusion.57 = (f32[512]{0:T(512)S(1)}, f32[512,512]{0,1:T(8,128)S(1)}) fusion(f32[512,512]{0,1:T(8,128)} %convolution_select_fusion, bf16[512,512]{1,0:T(8,128)(2,1)S(1)} %copy-done.8, s32[512]{0:T(512)S(1)} %bitcast.35), kind=kOutput, calls=%fused_computation.82 | convolution fusion | flops 269221376 | bytes 2625536 | tf_op jit(solution)/shard_map/dot_general | solution.py:102
  16.1 0.2 multiply_reduce_fusion.3
  16.3 0.2 copy.27
  16.5 0.2 copy-done.13
  16.7 0.0 copy-done.14
  16.7 0.4 fusion.12
  17.1 3.4 %fusion.54 = (f32[256]{0:T(256)S(1)}, f32[256]{0:T(256)S(1)}, f32[256,1280]{1,0:T(8,128)}) fusion(f32[256]{0:T(256)S(1)} %add_rsqrt_fusion.1, f32[256,1280]{1,0:T(8,128)} %copy-done.2, f32[256]{0:T(256)S(1)} %broadcast_multiply_fusion.5, f32[1280]{0:T(1024)S(1)} %copy-done.18, bf16[1280,512]{1,0:T(8,128)(2,1)S(1)} %copy-done, ...), kind=kOutput, calls=%fused_computation.79 | convolution fusion | flops 474480128 | bytes 5527040 | tf_op jit(solution)/shard_map/dot_general | solution.py:79
  20.6 2.2 %multiply_convert_fusion.1.rhs_b = bf16[256,1280]{1,0:T(8,128)(2,1)S(1)} fusion(f32[256,1280]{1,0:T(8,128)} %get-tuple-element.39, f32[256,1280]{1,0:T(8,128)} %copy-done.2, f32[256]{0:T(256)S(1)} %broadcast_multiply_fusion.3, f32[256]{0:T(256)S(1)} %broadcast_multiply_fusion.4, f32[256]{0:T(256)S(1)} %add_rsqrt_fusion.1, f32[256]{0:T(256)S(1)} %broadcast_multiply_fusion.5), kind=kLoop, calls=%fused_computation.19 | loop fusion | flops 2293760 | bytes 3280896 | tf_op jit(solution)/shard_map/convert_element_type | solution.py:80
  22.8 0.3 copy-done.21
  23.1 6.1 %fusion.rhs_a = bf16[256,2560]{1,0:T(8,128)(2,1)} fusion(bf16[256,1280]{1,0:T(8,128)(2,1)S(1)} %multiply_convert_fusion.1.rhs_b, bf16[2560,1280]{1,0:T(8,128)(2,1)} %param.26, f32[256,2560]{1,0:T(8,128)S(1)} %copy-done.21), kind=kOutput, calls=%fused_computation.3 | convolution fusion | flops 1684275200 | bytes 11141120 | tf_op jit(solution)/shard_map/dot_general | solution.py:81
  29.2 0.8 copy.28.inverse
  30.0 0.8 fusion.44.scatter
  30.8 0.6 broadcast_in_dim.42.gain
  31.4 94.6 %shard_map.201 = (bf16[160,2560]{1,0:T(8,128)(2,1)}, bf16[320,1280]{1,0:T(8,128)(2,1)}, bf16[512,1280]{1,0:T(8,128)(2,1)}) custom-call(bf16[256,1280]{1,0:T(8,128)(2,1)} %copy-done.3, bf16[256,2560]{1,0:T(8,128)(2,1)} %fusion.rhs_a, bf16[256,2560]{1,0:T(8,128)(2,1)} %copy-done.5, bf16[256,1280]{1,0:T(8,128)(2,1)} %copy-done.4, bf16[1280,2560]{1,0:T(8,128)(2,1)} %weight.1, ...), custom_call_target="tpu_custom_call" | custom-call | tf_op jit(solution)/shard_map/pallas_call | solution.py:384
  126.0 2.5 %convert_multiply_fusion = f32[320,1280]{1,0:T(8,128)} fusion(bf16[320,1280]{1,0:T(8,128)(2,1)} %get-tuple-element.9), kind=kLoop, calls=%fused_computation.14 | loop fusion | flops 819200 | bytes 2457600 | tf_op jit(solution)/shard_map/div | solution.py:504
  128.5 1.3 %convert_multiply_fusion.1 = f32[160,2560]{1,0:T(8,128)} fusion(bf16[160,2560]{1,0:T(8,128)(2,1)S(1)} %copy-done.7), kind=kLoop, calls=%fused_computation.15 | loop fusion | flops 819200 | bytes 2457600 | tf_op jit(solution)/shard_map/div | solution.py:504
  129.8 1.0 copy.29
  130.8 1.1 copy.31
  (50 shorter events, 0.2 us)
Async XLA Ops:
  0.6 11.1 %copy-start = (bf16[1280,512]{1,0:T(8,128)(2,1)S(1)}, bf16[1280,512]{1,0:T(8,128)(2,1)}, u32[]{:S(2)}) copy-start(bf16[1280,512]{1,0:T(8,128)(2,1)} %param.30) | copy-start | bytes 3932164
  2.3 2.4 %copy-start.10 = (f32[1280]{0:T(1024)S(1)}, f32[1280]{0:T(1024)}, u32[]{:S(2)}) copy-start(f32[1280]{0:T(1024)} %param.22) | copy-start | bytes 15364
  2.3 2.4 %copy-start.11 = (f32[1280]{0:T(1024)S(1)}, f32[1280]{0:T(1024)}, u32[]{:S(2)}) copy-start(f32[1280]{0:T(1024)} %param.23) | copy-start | bytes 15364
  2.3 3.8 %copy-start.1 = (bf16[1280,2560]{1,0:T(8,128)(2,1)S(1)}, bf16[1280,2560]{1,0:T(8,128)(2,1)}, u32[]{:S(2)}) copy-start(bf16[1280,2560]{1,0:T(8,128)(2,1)} %weight.1) | copy-start | bytes 19660804
  4.3 1.7 %copy-start.15 = (f32[2560]{0:T(1024)S(1)}, f32[2560]{0:T(1024)}, u32[]{:S(2)}) copy-start(f32[2560]{0:T(1024)} %param.25) | copy-start | bytes 30724
  4.7 4.7 %slice-start = ((s8[6553600]{0:T(1024)(128)(4,1)}), s8[4194304]{0:T(1024)(128)(4,1)S(1)}, s32[]{:S(2)}) async-start(s8[6553600]{0:T(1024)(128)(4,1)} %bitcast.36), calls=%async_computation | async-start | bytes 8388608
  6.0 3.3 %copy-start.3 = (bf16[256,1280]{1,0:T(8,128)(2,1)}, bf16[256,1280]{1,0:T(8,128)(2,1)S(1)}, u32[]{:S(2)}) copy-start(bf16[256,1280]{1,0:T(8,128)(2,1)S(1)} %get-tuple-element.26.lhs_a) | copy-start | bytes 1966084
  6.1 3.3 %slice-start.1 = ((s8[6553600]{0:T(1024)(128)(4,1)}), s8[2359296]{0:T(1024)(128)(4,1)S(1)}, s32[]{:S(2)}) async-start(s8[6553600]{0:T(1024)(128)(4,1)} %bitcast.36), calls=%async_computation.1 | async-start | bytes 4718592
  6.1 3.3 %copy-start.16 = (f32[1280]{0:T(1024)S(1)}, f32[1280]{0:T(1024)}, u32[]{:S(2)}) copy-start(f32[1280]{0:T(1024)} %param.27) | copy-start | bytes 15364
  9.4 2.0 %copy-start.5 = (bf16[256,2560]{1,0:T(8,128)(2,1)}, bf16[256,2560]{1,0:T(8,128)(2,1)S(1)}, u32[]{:S(2)}) copy-start(bf16[256,2560]{1,0:T(8,128)(2,1)S(1)} %get-tuple-element.33.lhs_b) | copy-start | bytes 3932164
  11.3 2.7 %copy-start.2 = (f32[256,1280]{1,0:T(8,128)}, f32[256,1280]{1,0:T(8,128)S(1)}, u32[]{:S(2)}) copy-start(f32[256,1280]{1,0:T(8,128)S(1)} %get-tuple-element.36) | copy-start | bytes 3932164
  11.3 0.7 copy-start.17
  11.4 0.8 copy-start.18
  11.4 0.8 copy-start.19
  11.4 0.8 copy-start.20
  12.2 1.9 %copy-start.8 = (bf16[512,512]{1,0:T(8,128)(2,1)S(1)}, bf16[512,512]{1,0:T(8,128)(2,1)}, u32[]{:S(2)}) copy-start(bf16[512,512]{1,0:T(8,128)(2,1)} %param.33) | copy-start | bytes 1572868
  12.2 1.9 %copy-start.12 = (s32[1,1,512]{2,1,0:T(1,128)S(1)}, s32[1,1,512]{2,1,0:T(1,128)}, u32[]{:S(2)}) copy-start(s32[1,1,512]{2,1,0:T(1,128)} %param.20) | copy-start | bytes 6148
  14.1 2.2 %copy-start.9 = (bf16[1,1,512,512]{3,2,1,0:T(8,128)(2,1)S(1)}, bf16[1,1,512,512]{3,2,1,0:T(8,128)(2,1)}, u32[]{:S(2)}) copy-start(bf16[1,1,512,512]{3,2,1,0:T(8,128)(2,1)} %param.21) | copy-start | bytes 1572868
  16.0 0.7 copy-start.13
  16.0 0.7 copy-start.14
  20.6 2.5 %copy-start.21 = (f32[256,2560]{1,0:T(8,128)S(1)}, f32[256,2560]{1,0:T(8,128)}, u32[]{:S(2)}) copy-start(f32[256,2560]{1,0:T(8,128)} %get-tuple-element.34) | copy-start | bytes 7864324
  22.8 6.4 %copy-start.4 = (bf16[256,1280]{1,0:T(8,128)(2,1)}, bf16[256,1280]{1,0:T(8,128)(2,1)S(1)}, u32[]{:S(2)}) copy-start(bf16[256,1280]{1,0:T(8,128)(2,1)S(1)} %multiply_convert_fusion.1.rhs_b) | copy-start | bytes 1966084
  126.0 2.5 %copy-start.7 = (bf16[160,2560]{1,0:T(8,128)(2,1)S(1)}, bf16[160,2560]{1,0:T(8,128)(2,1)}, u32[]{:S(2)}) copy-start(bf16[160,2560]{1,0:T(8,128)(2,1)} %get-tuple-element.8) | copy-start | bytes 2457604
  128.5 2.3 %copy-start.6 = (bf16[512,1280]{1,0:T(8,128)(2,1)S(1)}, bf16[512,1280]{1,0:T(8,128)(2,1)}, u32[]{:S(2)}) copy-start(bf16[512,1280]{1,0:T(8,128)(2,1)} %get-tuple-element.7) | copy-start | bytes 3932164

commit v5 on v4

--- a/solution.py
+++ b/solution.py
@@ -333,7 +333,7 @@
 
     stages = (stage0, stage1, stage2, stage3, stage4, stage5)
     for step in range(chunks + len(stages) - 1):
-        for at in reversed(range(len(stages))):
+        for at in (1, 0, 2, 3, 4, 5):
             j = step - at
             if 0 <= j < chunks:
                 for t in range(2):

time: 132 us -> 128 us (0.970)
  Pallas kernels: 94.6 us -> 90.4 us
    pallas_call x1, Pallas kernels: 94.6 us -> 90.4 us  [reduce_weights(): pl.pallas_call(functools.partial(reduce_kernel, chunks, z_count), out_sha...]
where the time goes in v5:
time: 128 us
  Pallas kernels  90.4 us (71%)
  matrix products  20.6 us (16%)
  other arithmetic  11.1 us (9%)
  local copies, waits for them, and re-layouts  4.8 us (4%)
    pallas_call x1, Pallas kernels, reduce_weights(): pl.pallas_call(functools.partial(reduce_kernel, chunks, z_count), out_sha...  90.4 us
    dot_general x1, matrix products, encode_back(): jnp.dot(grad_encoded, fc2_weight.T, preferred_element_type=jnp.float32)  6.08 us
    div x2, other arithmetic, shards(): fc1_grad, fc2_grad = [total / device_total for total in totals]  3.83 us
    dot_general x1, matrix products, encode_back(): jnp.dot(grad_compact, embed_weight.T, preferred_element_type=jnp.float32)  3.44 us
    unnamed x51, local copies, waits for them, and re-layouts  3.41 us
    dot_general x1, matrix products, encode(): jnp.dot(mlp_in, fc1_weight, preferred_element_type=jnp.float32) + fc1_bias  3.28 us

profile of v5, /device:TPU:0, one launch (start us, length us, event | category | flops | bytes accessed | tf_op | source)
XLA Modules:
  0.0 127.7 jit_solution(9836286799789925538)
XLA Ops:
  0.6 0.0 copy-start
  0.6 0.9 select_reduce_fusion
  1.6 0.7 broadcast_select_fusion
  2.3 2.1 %fusion.55 = (f32[256]{0:T(256)S(1)}, f32[256,1280]{1,0:T(8,128)S(1)}) fusion(bf16[1,1,512,1280]{3,2,1,0:T(8,128)(2,1)} %param.18, s32[512]{0:T(512)S(1)} %get-tuple-element.28), kind=kOutput, calls=%fused_computation.80 | convolution fusion | flops 336330496 | bytes 2624512 | tf_op jit(solution)/shard_map/dot_general | solution.py:470
  4.4 0.3 multiply_reduce_fusion.2
  4.7 1.4 %add_convert_fusion.1 = (bf16[256,1280]{1,0:T(8,128)(2,1)S(1)}, f32[256,1280]{1,0:T(8,128)}) fusion(f32[1280]{0:T(1024)S(1)} %copy-done.11, f32[1280]{0:T(1024)S(1)} %copy-done.10, f32[256]{0:T(256)S(1)} %add_rsqrt_fusion.2, f32[256,1280]{1,0:T(8,128)S(1)} %get-tuple-element.32, f32[256]{0:T(256)S(1)} %broadcast_multiply_fusion.6), kind=kLoop, calls=%fused_computation.23 | loop fusion | flops 1638400 | bytes 3289088 | tf_op jit(solution)/shard_map/convert_element_type | solution.py:51
  6.1 3.3 %multiply_convert_fusion = (bf16[256,2560]{1,0:T(8,128)(2,1)S(1)}, f32[256,2560]{1,0:T(8,128)}) fusion(f32[2560]{0:T(1024)S(1)} %copy-done.15, bf16[256,1280]{1,0:T(8,128)(2,1)S(1)} %get-tuple-element.26.lhs_a, bf16[1280,2560]{1,0:T(8,128)(2,1)S(1)} %copy-done.1), kind=kOutput, calls=%fused_computation.11 | convolution fusion | flops 1681653760 | bytes 11151360 | tf_op jit(solution)/shard_map/dot_general | solution.py:52
  9.4 1.9 %fusion.56 = (f32[256]{0:T(256)S(1)}, f32[256,1280]{1,0:T(8,128)S(1)}) fusion(f32[1280]{0:T(1024)S(1)} %copy-done.16, f32[256,1280]{1,0:T(8,128)S(1)} %get-tuple-element.32, bf16[256,2560]{1,0:T(8,128)(2,1)S(1)} %get-tuple-element.33.lhs_b, bf16[2560,1280]{1,0:T(8,128)(2,1)S(1)} %bitcast.37), kind=kOutput, calls=%fused_computation.81 | convolution fusion | flops 1678704384 | bytes 10491904 | tf_op jit(solution)/shard_map/dot_general | solution.py:55
  11.4 0.3 multiply_reduce_fusion.1
  11.7 0.4 copy-done.17
  12.1 0.1 copy-done.18
  12.1 0.0 copy-done.19
  12.2 0.1 copy-done.20
  12.2 1.9 %convolution_select_fusion = f32[512,512]{0,1:T(8,128)} fusion(bf16[1280,512]{1,0:T(8,128)(2,1)S(1)} %copy-done, f32[256,1280]{1,0:T(8,128)S(1)} %get-tuple-element.36, f32[1280]{0:T(1024)S(1)} %copy-done.17, f32[1280]{0:T(1024)S(1)} %copy-done.18, f32[256]{0:T(256)S(1)} %add_rsqrt_fusion.1, f32[256]{0:T(256)S(1)} %broadcast_multiply_fusion.5, ...), kind=kOutput, calls=%fused_computation.17 | convolution fusion | flops 472055808 | bytes 3688960 | tf_op jit(solution)/shard_map/dot_general | solution.py:472
  14.1 1.9 %fusion.57 = (f32[512]{0:T(512)S(1)}, f32[512,512]{0,1:T(8,128)S(1)}) fusion(f32[512,512]{0,1:T(8,128)} %convolution_select_fusion, bf16[512,512]{1,0:T(8,128)(2,1)S(1)} %copy-done.8, s32[512]{0:T(512)S(1)} %bitcast.35), kind=kOutput, calls=%fused_computation.82 | convolution fusion | flops 269221376 | bytes 2625536 | tf_op jit(solution)/shard_map/dot_general | solution.py:102
  16.1 0.2 multiply_reduce_fusion.3
  16.3 0.2 copy.27
  16.5 0.2 copy-done.13
  16.7 0.0 copy-done.14
  16.7 0.4 fusion.12
  17.1 3.4 %fusion.54 = (f32[256]{0:T(256)S(1)}, f32[256]{0:T(256)S(1)}, f32[256,1280]{1,0:T(8,128)}) fusion(f32[256]{0:T(256)S(1)} %add_rsqrt_fusion.1, f32[256,1280]{1,0:T(8,128)} %copy-done.2, f32[256]{0:T(256)S(1)} %broadcast_multiply_fusion.5, f32[1280]{0:T(1024)S(1)} %copy-done.18, bf16[1280,512]{1,0:T(8,128)(2,1)S(1)} %copy-done, ...), kind=kOutput, calls=%fused_computation.79 | convolution fusion | flops 474480128 | bytes 5527040 | tf_op jit(solution)/shard_map/dot_general | solution.py:79
  20.6 2.2 %multiply_convert_fusion.1.rhs_b = bf16[256,1280]{1,0:T(8,128)(2,1)S(1)} fusion(f32[256,1280]{1,0:T(8,128)} %get-tuple-element.39, f32[256,1280]{1,0:T(8,128)} %copy-done.2, f32[256]{0:T(256)S(1)} %broadcast_multiply_fusion.3, f32[256]{0:T(256)S(1)} %broadcast_multiply_fusion.4, f32[256]{0:T(256)S(1)} %add_rsqrt_fusion.1, f32[256]{0:T(256)S(1)} %broadcast_multiply_fusion.5), kind=kLoop, calls=%fused_computation.19 | loop fusion | flops 2293760 | bytes 3280896 | tf_op jit(solution)/shard_map/convert_element_type | solution.py:80
  22.8 0.3 copy-done.21
  23.1 6.1 %fusion.rhs_a = bf16[256,2560]{1,0:T(8,128)(2,1)} fusion(bf16[256,1280]{1,0:T(8,128)(2,1)S(1)} %multiply_convert_fusion.1.rhs_b, bf16[2560,1280]{1,0:T(8,128)(2,1)} %param.26, f32[256,2560]{1,0:T(8,128)S(1)} %copy-done.21), kind=kOutput, calls=%fused_computation.3 | convolution fusion | flops 1684275200 | bytes 11141120 | tf_op jit(solution)/shard_map/dot_general | solution.py:81
  29.2 0.8 copy.28.inverse
  30.0 0.8 fusion.44.scatter
  30.8 0.6 broadcast_in_dim.42.gain
  31.4 90.4 %shard_map.201 = (bf16[160,2560]{1,0:T(8,128)(2,1)}, bf16[320,1280]{1,0:T(8,128)(2,1)}, bf16[512,1280]{1,0:T(8,128)(2,1)}) custom-call(bf16[256,1280]{1,0:T(8,128)(2,1)} %copy-done.3, bf16[256,2560]{1,0:T(8,128)(2,1)} %fusion.rhs_a, bf16[256,2560]{1,0:T(8,128)(2,1)} %copy-done.5, bf16[256,1280]{1,0:T(8,128)(2,1)} %copy-done.4, bf16[1280,2560]{1,0:T(8,128)(2,1)} %weight.1, ...), custom_call_target="tpu_custom_call" | custom-call | tf_op jit(solution)/shard_map/pallas_call | solution.py:384
  121.8 2.5 %convert_multiply_fusion = f32[320,1280]{1,0:T(8,128)} fusion(bf16[320,1280]{1,0:T(8,128)(2,1)} %get-tuple-element.9), kind=kLoop, calls=%fused_computation.14 | loop fusion | flops 819200 | bytes 2457600 | tf_op jit(solution)/shard_map/div | solution.py:504
  124.3 1.3 %convert_multiply_fusion.1 = f32[160,2560]{1,0:T(8,128)} fusion(bf16[160,2560]{1,0:T(8,128)(2,1)S(1)} %copy-done.7), kind=kLoop, calls=%fused_computation.15 | loop fusion | flops 819200 | bytes 2457600 | tf_op jit(solution)/shard_map/div | solution.py:504
  125.6 1.0 copy.29
  126.6 1.1 copy.31
  (50 shorter events, 0.2 us)
Async XLA Ops:
  0.6 11.1 %copy-start = (bf16[1280,512]{1,0:T(8,128)(2,1)S(1)}, bf16[1280,512]{1,0:T(8,128)(2,1)}, u32[]{:S(2)}) copy-start(bf16[1280,512]{1,0:T(8,128)(2,1)} %param.30) | copy-start | bytes 3932164
  2.3 2.4 %copy-start.10 = (f32[1280]{0:T(1024)S(1)}, f32[1280]{0:T(1024)}, u32[]{:S(2)}) copy-start(f32[1280]{0:T(1024)} %param.22) | copy-start | bytes 15364
  2.3 2.4 %copy-start.11 = (f32[1280]{0:T(1024)S(1)}, f32[1280]{0:T(1024)}, u32[]{:S(2)}) copy-start(f32[1280]{0:T(1024)} %param.23) | copy-start | bytes 15364
  2.3 3.8 %copy-start.1 = (bf16[1280,2560]{1,0:T(8,128)(2,1)S(1)}, bf16[1280,2560]{1,0:T(8,128)(2,1)}, u32[]{:S(2)}) copy-start(bf16[1280,2560]{1,0:T(8,128)(2,1)} %weight.1) | copy-start | bytes 19660804
  4.3 1.7 %copy-start.15 = (f32[2560]{0:T(1024)S(1)}, f32[2560]{0:T(1024)}, u32[]{:S(2)}) copy-start(f32[2560]{0:T(1024)} %param.25) | copy-start | bytes 30724
  4.7 4.7 %slice-start = ((s8[6553600]{0:T(1024)(128)(4,1)}), s8[4194304]{0:T(1024)(128)(4,1)S(1)}, s32[]{:S(2)}) async-start(s8[6553600]{0:T(1024)(128)(4,1)} %bitcast.36), calls=%async_computation | async-start | bytes 8388608
  6.0 3.3 %copy-start.3 = (bf16[256,1280]{1,0:T(8,128)(2,1)}, bf16[256,1280]{1,0:T(8,128)(2,1)S(1)}, u32[]{:S(2)}) copy-start(bf16[256,1280]{1,0:T(8,128)(2,1)S(1)} %get-tuple-element.26.lhs_a) | copy-start | bytes 1966084
  6.1 3.3 %slice-start.1 = ((s8[6553600]{0:T(1024)(128)(4,1)}), s8[2359296]{0:T(1024)(128)(4,1)S(1)}, s32[]{:S(2)}) async-start(s8[6553600]{0:T(1024)(128)(4,1)} %bitcast.36), calls=%async_computation.1 | async-start | bytes 4718592
  6.1 3.3 %copy-start.16 = (f32[1280]{0:T(1024)S(1)}, f32[1280]{0:T(1024)}, u32[]{:S(2)}) copy-start(f32[1280]{0:T(1024)} %param.27) | copy-start | bytes 15364
  9.4 2.0 %copy-start.5 = (bf16[256,2560]{1,0:T(8,128)(2,1)}, bf16[256,2560]{1,0:T(8,128)(2,1)S(1)}, u32[]{:S(2)}) copy-start(bf16[256,2560]{1,0:T(8,128)(2,1)S(1)} %get-tuple-element.33.lhs_b) | copy-start | bytes 3932164
  11.3 2.7 %copy-start.2 = (f32[256,1280]{1,0:T(8,128)}, f32[256,1280]{1,0:T(8,128)S(1)}, u32[]{:S(2)}) copy-start(f32[256,1280]{1,0:T(8,128)S(1)} %get-tuple-element.36) | copy-start | bytes 3932164
  11.3 0.7 copy-start.17
  11.4 0.8 copy-start.18
  11.4 0.8 copy-start.19
  11.4 0.8 copy-start.20
  12.2 1.9 %copy-start.8 = (bf16[512,512]{1,0:T(8,128)(2,1)S(1)}, bf16[512,512]{1,0:T(8,128)(2,1)}, u32[]{:S(2)}) copy-start(bf16[512,512]{1,0:T(8,128)(2,1)} %param.33) | copy-start | bytes 1572868
  12.2 1.9 %copy-start.12 = (s32[1,1,512]{2,1,0:T(1,128)S(1)}, s32[1,1,512]{2,1,0:T(1,128)}, u32[]{:S(2)}) copy-start(s32[1,1,512]{2,1,0:T(1,128)} %param.20) | copy-start | bytes 6148
  14.1 2.2 %copy-start.9 = (bf16[1,1,512,512]{3,2,1,0:T(8,128)(2,1)S(1)}, bf16[1,1,512,512]{3,2,1,0:T(8,128)(2,1)}, u32[]{:S(2)}) copy-start(bf16[1,1,512,512]{3,2,1,0:T(8,128)(2,1)} %param.21) | copy-start | bytes 1572868
  16.0 0.7 copy-start.13
  16.0 0.7 copy-start.14
  20.6 2.5 %copy-start.21 = (f32[256,2560]{1,0:T(8,128)S(1)}, f32[256,2560]{1,0:T(8,128)}, u32[]{:S(2)}) copy-start(f32[256,2560]{1,0:T(8,128)} %get-tuple-element.34) | copy-start | bytes 7864324
  22.8 6.4 %copy-start.4 = (bf16[256,1280]{1,0:T(8,128)(2,1)}, bf16[256,1280]{1,0:T(8,128)(2,1)S(1)}, u32[]{:S(2)}) copy-start(bf16[256,1280]{1,0:T(8,128)(2,1)S(1)} %multiply_convert_fusion.1.rhs_b) | copy-start | bytes 1966084
  121.8 2.5 %copy-start.7 = (bf16[160,2560]{1,0:T(8,128)(2,1)S(1)}, bf16[160,2560]{1,0:T(8,128)(2,1)}, u32[]{:S(2)}) copy-start(bf16[160,2560]{1,0:T(8,128)(2,1)} %get-tuple-element.8) | copy-start | bytes 2457604
  124.3 2.3 %copy-start.6 = (bf16[512,1280]{1,0:T(8,128)(2,1)S(1)}, bf16[512,1280]{1,0:T(8,128)(2,1)}, u32[]{:S(2)}) copy-start(bf16[512,1280]{1,0:T(8,128)(2,1)} %get-tuple-element.7) | copy-start | bytes 3932164
